TPU v7x, 32 devices: a whole 2x2x4 slice. The times are simulated.
32 devices in a mesh: dp: 16 (over z, y, x), section: 2 (over core).
Axes of the slice: x: 2, y: 2, z: 4, core: 2. Of those that a mesh axis runs over, the one named last changes fastest.
Arguments:
- acts: bfloat16 [2, 2, 2048, 2048], P('section', None, 'dp'), may hold values from -6 to 6
- cotan: bfloat16 [2, 2, 2048, 384], P('section', None, 'dp'), may hold values from -0.09375 to 0.09375
- counts: int32 [2, 2, 16, 1], P('section', None, 'dp'), may hold values from 32 to 128
- weight: float32 [2, 786432], P('section', 'dp'), may hold values from -4 to 4
- moment: float32 [2, 786432], P('section', 'dp'), may hold values from -4 to 4
- second: float32 [2, 786432], P('section', 'dp'), may hold values from 0.1 to 1
Outputs:
- new_weight: float32 [2, 786432], P('section', 'dp')
- new_moment: float32 [2, 786432], P('section', 'dp')
- new_second: float32 [2, 786432], P('section', 'dp')
All inputs are finite; a program needn't handle non-finite values.
Results may differ from a plain program's by a relative error of at most 0.0003.
Values sent between devices are 32-bit elements; how exact they have to be, the bound alone decides.
A program may use at most 64 MiB of HBM per device.

v0:
```python
import functools
import jax
import jax.numpy as jnp
from jax import lax
from jax.experimental import pallas as pl
from jax.experimental.pallas import tpu as pltpu
from jax.sharding import PartitionSpec as P

LANES = 128
MESH = pl.DeviceIdType.MESH


def adamw_shard(grad, weight_now, moment_now, second_now):
    new_m = 0.9 * moment_now + 0.1 * grad
    new_v = 0.95 * second_now + 0.05 * grad * grad
    corr_m = new_m / (1.0 - 0.9**10)
    corr_v = new_v / (1.0 - 0.95**10)
    new_w = weight_now - 0.01 * (corr_m / (jnp.sqrt(corr_v) + 1e-08) + 0.1 * weight_now)
    return (new_w, new_m, new_v)


def adamw_kernel(grad, weight, moment, second, new_weight, new_moment, new_second):
    new_w, new_m, new_v = adamw_shard(grad[...], weight[...], moment[...], second[...])
    new_weight[...] = new_w
    new_moment[...] = new_m
    new_second[...] = new_v


def dp_digits(mesh):
    size = mesh.shape["dp"]
    line = mesh.devices.reshape(size, -1)[:, 0]
    digits = []
    if hasattr(line[0], "coords"):
        for axis in range(3):
            at = [device.coords[axis] for device in line]
            if len(set(at)) > 1:
                digits.append((len(set(at)), next(j for j in range(size) if at[j] != at[0])))
    total = 1
    for count, stride in digits:
        total *= count
    if total != size:
        digits = [(size, 1)] if size > 1 else []
    digits.sort()
    return [(1, 1)] * (3 - len(digits)) + digits


def axis_orders(digits):
    a, b, c = digits
    return [(a, b, c), (b, a, c), (c, a, b), (c, b, a)]


def row_spans(shard_rows):
    late = shard_rows // 128 * 8
    early = (shard_rows - 2 * late) // 2
    spans = [(0, early), (early, early), (2 * early, late), (2 * early + late, late)]
    return spans[:4 if late else 2]


def reduce_kernel(digits, micro, pieces, acts, cotan, counts, out, acts_held, cotan_held, acts_out, cotan_out, acts_in, cotan_in, rhs,
                  grad, got1, got2, got3, load_sem, part_send, part_recv, send1, recv1, send2, recv2, send3, recv3):
    sections = lax.axis_size("section")
    section = lax.axis_index("section")
    dp = lax.axis_index("dp")
    mirror = sections - 1 - section

    def moved(step, digit):
        count, stride = digit
        mine = lax.rem(lax.div(dp, stride), count)
        return (lax.rem(mine + step, count) - mine) * stride

    peers = [(dp, mirror)]
    for digit in digits:
        peers += [(dp + moved(step, digit), section) for step in range(1, digit[0])]
    barrier = pltpu.get_barrier_semaphore()
    for peer in peers:
        pl.semaphore_signal(barrier, inc=1, device_id=peer, device_id_type=MESH)
    loads = [
        pltpu.make_async_copy(cotan, cotan_held, load_sem.at[0]),
        pltpu.make_async_copy(acts.at[1], acts_held.at[1], load_sem.at[1]),
        pltpu.make_async_copy(acts.at[0], acts_held.at[0], load_sem.at[2]),
    ]
    for load in loads:
        load.start()

    rows, depth = acts.shape[1], acts.shape[2]
    width = cotan.shape[2]
    slots = rows // micro
    shard_rows = out.shape[0]
    orders = axis_orders(digits)
    spans = row_spans(shard_rows)
    last = digits[2]
    per_row = width // LANES

    def masked(k):
        parts = []
        for b in range(micro):
            block = cotan_held[k, b * slots:(b + 1) * slots, :].astype(jnp.float32)
            place = lax.broadcasted_iota(jnp.int32, (slots, width), 0)
            parts.append(jnp.where(place < counts[b, k], block, 0.0))
        return parts[0] if micro == 1 else jnp.concatenate(parts, axis=0)

    steps3 = sorted(range(1, last[0]), key=lambda step: -min(step, last[0] - step)) + [0]
    piece = depth // pieces
    by_owner = pieces == lax.axis_size("dp")
    kinds = {"forward": [], "own": [], "mine": []}
    for step_a in range(digits[0][0]):
        for step_b in range(digits[1][0]):
            kind = "forward" if step_a and step_b else "own" if step_a or step_b else "mine"
            kinds[kind].append((step_a, step_b))
    groups = [("forward", 0), ("own", 0), ("forward", 1)]
    groups += [(kind, i) for i in range(len(steps3)) for kind in ("own", "forward", "mine") if (kind, i) not in groups]
    owners, places, group_of = [], [], {}
    for kind, i in groups:
        if i < len(steps3):
            group_of[kind, i] = range(len(owners), len(owners) + len(kinds[kind]))
            for step_a, step_b in kinds[kind]:
                places.append((step_a, step_b, steps3[i]))
                owners.append(dp + moved(step_a, digits[0]) + moved(step_b, digits[1]) + moved(steps3[i], last))
    if not by_owner:
        owners = list(range(pieces))

    def columns(at):
        start = owners[at] * piece
        return pl.ds(start if isinstance(start, int) else pl.multiple_of(start, LANES), piece)

    def to_mirror(src, dst, at):
        return pltpu.make_async_remote_copy(
            src_ref=src, dst_ref=dst, send_sem=part_send.at[at], recv_sem=part_recv.at[at],
            device_id=(dp, mirror), device_id_type=MESH)

    exchange = [to_mirror(acts_out.at[at], acts_in.at[at], at) for at in range(pieces)]
    exchange.append(to_mirror(cotan_out, cotan_in, pieces))
    loads[0].wait()
    cotan_out[...] = masked(1)
    rhs[0:rows, :] = masked(0).astype(jnp.bfloat16)
    loads[1].wait()
    for at in range(pieces):
        acts_out[at] = acts_held[1, :, columns(at)].astype(jnp.float32)
    pl.semaphore_wait(barrier, len(peers))
    exchange[pieces].start()
    for copy in exchange[:pieces]:
        copy.start()
    loads[2].wait()
    exchange[pieces].wait_recv()
    rhs[rows:2 * rows, :] = cotan_in[...].astype(jnp.bfloat16)

    def make(at):
        exchange[at].wait_recv()
        lhs = jnp.concatenate([acts_held[0, :, columns(at)], acts_in[at].astype(jnp.bfloat16)], axis=0)
        product = lax.dot_general(lhs, rhs[...], (((0,), (0,)), ((), ())), preferred_element_type=jnp.float32)
        first = owners[at] * (piece * per_row)
        if not isinstance(first, int):
            first = pl.multiple_of(first, 8)
        for c in range(per_row):
            grad[pl.ds(first + c, piece, stride=per_row), :] = product[:, c * LANES:(c + 1) * LANES]

    def make_group(kind, i):
        if by_owner and (kind, i) in group_of:
            for at in group_of.pop((kind, i)):
                make(at)
                made.append(places[at])

    made = []
    if not by_owner:
        for at in range(pieces):
            make(at)
        made += places

    def block(o, step1, step2, step3):
        first, second, third = orders[o]
        owner = dp + moved(step1, first) + moved(step2, second) + moved(step3, third)
        return grad.at[pl.ds(pl.multiple_of(owner * shard_rows + spans[o][0], 8), spans[o][1]), :]

    def base1(o, step1, step2, step3):
        first, second, third = orders[o]
        return ((step1 - 1) * second[0] + step2) * third[0] + step3

    def stage1(o, step1, step2, step3):
        at = base1(o, step1, step2, step3)
        return pltpu.make_async_remote_copy(
            src_ref=block(o, step1, step2, step3), dst_ref=got1[o].at[at], send_sem=send1[o].at[at], recv_sem=recv1[o].at[at],
            device_id=(dp + moved(step1, orders[o][0]), section), device_id_type=MESH)

    def stage2(o, step2, step3):
        at = (step2 - 1) * orders[o][2][0] + step3
        return pltpu.make_async_remote_copy(
            src_ref=block(o, 0, step2, step3), dst_ref=got2[o].at[at], send_sem=send2[o].at[at], recv_sem=recv2[o].at[at],
            device_id=(dp + moved(step2, orders[o][1]), section), device_id_type=MESH)

    def stage3(o, step3):
        at = step3 - 1
        return pltpu.make_async_remote_copy(
            src_ref=block(o, 0, 0, step3), dst_ref=got3[o].at[at], send_sem=send3[o].at[at], recv_sem=recv3[o].at[at],
            device_id=(dp + moved(step3, orders[o][2]), section), device_id_type=MESH)

    started = []

    def start(copy):
        copy.start()
        started.append(copy)

    def arrived1(o, step2, step3):
        total = block(o, 0, step2, step3)[...]
        for step1 in range(1, orders[o][0][0]):
            stage1(o, step1, step2, step3).wait_recv()
            total += got1[o][base1(o, step1, step2, step3)]
        return total

    def arrived2(o, step3):
        total = arrived1(o, 0, step3)
        for step2 in range(1, orders[o][1][0]):
            stage2(o, step2, step3).wait_recv()
            total += got2[o][(step2 - 1) * orders[o][2][0] + step3]
        return total

    def send_forward(i):
        if i < len(steps3):
            for o in range(2):
                for step1 in range(1, orders[o][0][0]):
                    for step2 in range(1, orders[o][1][0]):
                        start(stage1(o, step1, step2, steps3[i]))

    def send_own(i):
        if i < len(steps3):
            for o in range(2):
                for step1 in range(1, orders[o][0][0]):
                    start(stage1(o, step1, 0, steps3[i]))

    def send_second(i):
        for o in range(2):
            for step2 in range(1, orders[o][1][0]):
                block(o, 0, step2, steps3[i])[...] = arrived1(o, step2, steps3[i])
                start(stage2(o, step2, steps3[i]))

    def send_third(i):
        for o in range(2):
            block(o, 0, 0, steps3[i])[...] = arrived2(o, steps3[i])
            start(stage3(o, steps3[i]))

    late = range(2, len(spans))

    def late_first(step2, step3, step1):
        for o in late:
            if step1:
                start(stage1(o, step1, *((step2, step3) if orders[o][1] is digits[0] else (step3, step2))))

    def late_second():
        for o in late:
            for step2 in range(1, orders[o][1][0]):
                for step3 in reversed(range(orders[o][2][0])):
                    block(o, 0, step2, step3)[...] = arrived1(o, step2, step3)
                    start(stage2(o, step2, step3))

    def late_third():
        for o in late:
            for step3 in range(1, orders[o][2][0]):
                block(o, 0, 0, step3)[...] = arrived2(o, step3)
                start(stage3(o, step3))

    def send_late():
        while made:
            late_first(*made.pop(0))

    end = len(steps3) - 1
    make_group("forward", 0)
    send_forward(0)
    make_group("own", 0)
    send_own(0)
    send_late()
    make_group("forward", 1)
    if end > 1:
        send_forward(1)
    send_late()
    for kind, i in list(group_of):
        make_group(kind, i)
        send_late()
    for i in range(end + 1):
        if i == end and i:
            send_third(i - 1)
        send_second(i)
        if i == end - 1:
            send_forward(end)
        send_own(i + 1)
        if i + 2 < end:
            send_forward(i + 2)
        if 1 <= i < end:
            send_third(i - 1)
        if i == end - 2:
            late_second()
        if i == end - 1:
            late_third()
    if len(steps3) < 3:
        late_second()
    if len(steps3) < 2:
        late_third()
    for o in reversed(range(len(spans))):
        total = arrived2(o, 0)
        for step3 in range(1, orders[o][2][0]):
            stage3(o, step3).wait_recv()
            total += got3[o][step3 - 1]
        out[spans[o][0]:spans[o][0] + spans[o][1], :] = total
    for copy in exchange + started:
        copy.wait_send()


def shards(digits, acts, cotan, counts, weight, moment, second):
    micro = counts.shape[3]
    rows, depth = acts.shape[2], acts.shape[3]
    width = cotan.shape[3]
    shard_rows = weight.shape[1] // LANES
    piece = weight.shape[1] // width
    pieces = depth // piece if piece % LANES == 0 and weight.shape[1] % width == 0 else depth // (2 * LANES)
    orders = axis_orders(digits)
    spans = row_spans(shard_rows)
    orders = orders[:len(spans)]
    counts1 = [(first[0] - 1) * second[0] * third[0] for first, second, third in orders]
    counts2 = [(second[0] - 1) * third[0] for first, second, third in orders]
    counts3 = [third[0] - 1 for first, second, third in orders]

    def buffers(sizes):
        return [pltpu.VMEM((max(size, 1), span[1], LANES), jnp.float32) for size, span in zip(sizes, spans)]

    def semaphores(sizes):
        return [pltpu.SemaphoreType.DMA((max(size, 1),)) for size in sizes]

    hbm = pl.BlockSpec(memory_space=pl.ANY)
    vmem = pl.BlockSpec(memory_space=pltpu.VMEM)
    shard = pl.pallas_call(
        functools.partial(reduce_kernel, digits, micro, pieces),
        out_shape=jax.ShapeDtypeStruct((shard_rows, LANES), jnp.float32),
        in_specs=[hbm, hbm, pl.BlockSpec(memory_space=pltpu.SMEM)],
        out_specs=vmem,
        scratch_shapes=[
            pltpu.VMEM((2, rows, depth), jnp.bfloat16),
            pltpu.VMEM((2, rows, width), jnp.bfloat16),
            pltpu.VMEM((pieces, rows, depth // pieces), jnp.float32),
            pltpu.VMEM((rows, width), jnp.float32),
            pltpu.VMEM((pieces, rows, depth // pieces), jnp.float32),
            pltpu.VMEM((rows, width), jnp.float32),
            pltpu.VMEM((2 * rows, width), jnp.bfloat16),
            pltpu.VMEM((depth * width // LANES, LANES), jnp.float32),
            buffers(counts1), buffers(counts2), buffers(counts3),
            pltpu.SemaphoreType.DMA((3,)), pltpu.SemaphoreType.DMA((pieces + 1,)), pltpu.SemaphoreType.DMA((pieces + 1,)),
            semaphores(counts1), semaphores(counts1), semaphores(counts2), semaphores(counts2),
            semaphores(counts3), semaphores(counts3),
        ],
        compiler_params=pltpu.CompilerParams(collective_id=0, has_side_effects=True),
        name="reduce_grad",
    )(acts[0], cotan[0], counts[0, :, 0, :].T)
    flat = jax.ShapeDtypeStruct((shard_rows, LANES), jnp.float32)
    outs = pl.pallas_call(
        adamw_kernel,
        out_shape=(flat, flat, flat),
        in_specs=[vmem] * 4,
        out_specs=(vmem, vmem, vmem),
        name="adamw",
    )(shard, *(array.reshape(shard_rows, LANES) for array in (weight, moment, second)))
    return tuple(array.reshape(weight.shape) for array in outs)


def solution(mesh):
    in_specs = (
        P("section", None, "dp", None),
        P("section", None, "dp", None),
        P("section", None, "dp", None),
        P("section", "dp"),
        P("section", "dp"),
        P("section", "dp"),
    )
    out_specs = (P("section", "dp"), P("section", "dp"), P("section", "dp"))
    body = functools.partial(shards, dp_digits(mesh))
    return jax.shard_map(body, mesh=mesh, in_specs=in_specs, out_specs=out_specs, check_vma=False)
```

profile of v0, /device:TPU:0, one launch (start us, length us, event | category | flops | bytes accessed | tf_op | source)
XLA Modules:
  0.0 38.6 jit_solution(3262755187132070482)
XLA Ops:
  0.6 35.8 %reduce_grad.1.grad = f32[384,128]{1,0:T(8,128)} custom-call(bf16[2,128,2048]{2,1,0:T(8,128)(2,1)} %bitcast.9, bf16[2,128,384]{2,1,0:T(8,128)(2,1)} %bitcast.13, s32[1,2]{1,0:T(1,128)} %bitcast.14), custom_call_target="tpu_custom_call" | custom-call | tf_op jit(solution)/shard_map/reduce_grad/pallas_call | solution.py:328
  36.4 2.2 %adamw.1 = (f32[384,128]{1,0:T(8,128)}, f32[384,128]{1,0:T(8,128)}, f32[384,128]{1,0:T(8,128)}) custom-call(f32[384,128]{1,0:T(8,128)} %reduce_grad.1.grad, f32[384,128]{1,0:T(8,128)} %bitcast.10, f32[384,128]{1,0:T(8,128)} %bitcast.11, f32[384,128]{1,0:T(8,128)} %bitcast.12), custom_call_target="tpu_custom_call" | custom-call | tf_op jit(solution)/shard_map/adamw/pallas_call | solution.py:351
where the time goes:
time: 38.8 us; the launch traced here: 38.6 us
  Pallas kernels  38 us (98%)
  between operations  0.64 us (2%)
    pallas_call x1, Pallas kernels, shards(): pl.pallas_call(functools.partial(reduce_kernel, digits, micro, pieces), o...  35.8 us
    pallas_call x1, Pallas kernels, shards(): pl.pallas_call(adamw_kernel, out_shape=(flat, flat, flat), in_specs=[vmem...  2.15 us

commit v1 on v0

--- a/solution.py
+++ b/solution.py
@@ -8,6 +8,67 @@
 
 LANES = 128
 MESH = pl.DeviceIdType.MESH
+
+
+CHUNKS = {"A": (7,), "B": (7,), "C": (1,), "D": (1,)}
+FINALS = (("C", 0), ("D", 0), ("A", 0), ("B", 0))
+ORDERS = (
+    (
+        ("1", "A", 0, 1, 3), ("1", "B", 0, 1, 3), ("z", "C", 0, 1, 1, 3), ("z", "D", 0, 1, 1, 3), ("z", "C", 0, 1, 1, 2),
+        ("z", "D", 0, 1, 1, 2), ("z", "C", 0, 1, 1, 1), ("z", "C", 0, 0, 1, 3), ("z", "C", 0, 1, 0, 3), ("1", "A", 0, 1, 2),
+        ("1", "A", 0, 1, 1), ("1", "B", 0, 1, 2), ("z", "D", 0, 0, 1, 3), ("z", "D", 0, 1, 0, 3), ("z", "C", 0, 0, 1, 2),
+        ("z", "C", 0, 1, 0, 2), ("z", "D", 0, 1, 1, 1), ("z", "C", 0, 0, 0, 3), ("z", "D", 0, 0, 1, 2), ("1", "B", 0, 1, 1),
+        ("1", "B", 0, 0, 3), ("z", "D", 0, 1, 0, 2), ("z", "D", 0, 0, 0, 3), ("z", "C", 0, 0, 1, 1), ("z", "C", 0, 1, 0, 1),
+        ("z", "C", 0, 0, 0, 2), ("z", "D", 0, 0, 1, 1), ("z", "D", 0, 1, 0, 1), ("1", "A", 0, 0, 3), ("2", "B", 0, 3),
+        ("z", "D", 0, 0, 0, 2), ("z", "C", 0, 0, 0, 1), ("z", "D", 0, 0, 0, 1), ("2", "A", 0, 3), ("1", "A", 0, 0, 2),
+        ("2", "B", 0, 2), ("2", "A", 0, 2), ("1", "B", 0, 0, 2), ("3", "B", 0, 3), ("1", "A", 0, 1, 0), ("1", "A", 0, 0, 1),
+        ("2", "A", 0, 1), ("3", "A", 0, 3), ("1", "B", 0, 1, 0), ("3", "A", 0, 2), ("2", "B", 0, 1), ("x", "C", 0, 1),
+        ("1", "B", 0, 0, 1), ("3", "B", 0, 2), ("x", "D", 0, 1), ("1", "A", 0, 0, 0), ("x", "C", 0, 0), ("2", "A", 0, 0),
+        ("3", "A", 0, 1), ("1", "B", 0, 0, 0), ("2", "B", 0, 0), ("3", "B", 0, 1), ("y", "C", 0), ("y", "D", 0),
+        ("x", "D", 0, 0),
+    ),
+    (
+        ("1", "A", 0, 1, 3), ("1", "B", 0, 1, 3), ("1", "A", 0, 1, 0), ("1", "A", 0, 1, 2), ("1", "B", 0, 1, 0),
+        ("z", "C", 0, 1, 1, 3), ("z", "D", 0, 1, 1, 3), ("z", "C", 0, 1, 1, 2), ("z", "D", 0, 1, 1, 2), ("1", "B", 0, 1, 2),
+        ("z", "C", 0, 0, 1, 3), ("z", "C", 0, 1, 0, 3), ("z", "D", 0, 0, 1, 3), ("z", "D", 0, 1, 0, 3), ("z", "C", 0, 0, 1, 2),
+        ("z", "C", 0, 1, 0, 2), ("1", "A", 0, 0, 3), ("2", "B", 0, 3), ("2", "A", 0, 3), ("z", "C", 0, 0, 0, 3),
+        ("z", "D", 0, 0, 1, 2), ("z", "D", 0, 1, 0, 2), ("z", "D", 0, 0, 0, 3), ("z", "C", 0, 0, 0, 2), ("1", "B", 0, 0, 3),
+        ("z", "D", 0, 0, 0, 2), ("z", "C", 0, 1, 1, 0), ("z", "D", 0, 1, 1, 0), ("1", "A", 0, 0, 0), ("1", "A", 0, 1, 1),
+        ("2", "A", 0, 0), ("z", "C", 0, 0, 1, 0), ("z", "C", 0, 1, 0, 0), ("z", "D", 0, 0, 1, 0), ("z", "D", 0, 1, 0, 0),
+        ("3", "A", 0, 3), ("2", "A", 0, 2), ("z", "C", 0, 0, 0, 0), ("z", "D", 0, 0, 0, 0), ("1", "A", 0, 0, 2),
+        ("2", "B", 0, 0), ("1", "B", 0, 0, 0), ("1", "B", 0, 1, 1), ("2", "B", 0, 2), ("x", "C", 0, 1), ("1", "B", 0, 0, 2),
+        ("x", "D", 0, 1), ("1", "A", 0, 0, 1), ("x", "C", 0, 0), ("2", "A", 0, 1), ("3", "A", 0, 0), ("3", "B", 0, 3),
+        ("1", "B", 0, 0, 1), ("2", "B", 0, 1), ("3", "B", 0, 0), ("3", "A", 0, 2), ("y", "C", 0), ("y", "D", 0),
+        ("x", "D", 0, 0), ("3", "B", 0, 2),
+    ),
+    (
+        ("1", "A", 0, 1, 0), ("1", "B", 0, 1, 0), ("1", "A", 0, 1, 1), ("1", "A", 0, 1, 3), ("1", "B", 0, 1, 1),
+        ("1", "B", 0, 1, 3), ("z", "C", 0, 1, 1, 3), ("z", "C", 0, 1, 1, 0), ("z", "D", 0, 1, 1, 3), ("z", "D", 0, 1, 1, 0),
+        ("z", "C", 0, 1, 1, 1), ("z", "D", 0, 1, 1, 1), ("1", "A", 0, 0, 0), ("2", "B", 0, 0), ("2", "A", 0, 0),
+        ("z", "C", 0, 0, 1, 3), ("z", "C", 0, 0, 1, 0), ("z", "C", 0, 1, 0, 3), ("z", "C", 0, 1, 0, 0), ("z", "D", 0, 0, 1, 3),
+        ("z", "D", 0, 0, 1, 0), ("z", "D", 0, 1, 0, 3), ("z", "D", 0, 1, 0, 0), ("z", "C", 0, 0, 1, 1), ("z", "C", 0, 1, 0, 1),
+        ("1", "B", 0, 0, 0), ("z", "D", 0, 0, 1, 1), ("z", "C", 0, 0, 0, 3), ("z", "C", 0, 0, 0, 0), ("z", "D", 0, 0, 0, 0),
+        ("z", "D", 0, 1, 0, 1), ("z", "D", 0, 0, 0, 3), ("z", "C", 0, 0, 0, 1), ("1", "A", 0, 0, 1), ("1", "A", 0, 1, 2),
+        ("2", "A", 0, 1), ("z", "D", 0, 0, 0, 1), ("3", "A", 0, 0), ("2", "A", 0, 3), ("3", "B", 0, 0), ("1", "A", 0, 0, 3),
+        ("2", "B", 0, 1), ("1", "B", 0, 0, 1), ("1", "B", 0, 1, 2), ("2", "B", 0, 3), ("x", "C", 0, 1), ("1", "B", 0, 0, 3),
+        ("3", "A", 0, 3), ("x", "D", 0, 1), ("1", "A", 0, 0, 2), ("x", "C", 0, 0), ("2", "A", 0, 2), ("1", "B", 0, 0, 2),
+        ("2", "B", 0, 2), ("3", "A", 0, 1), ("3", "B", 0, 3), ("y", "C", 0), ("y", "D", 0), ("x", "D", 0, 0), ("3", "B", 0, 1),
+    ),
+    (
+        ("1", "A", 0, 1, 0), ("1", "B", 0, 1, 0), ("z", "C", 0, 1, 1, 0), ("z", "D", 0, 1, 1, 0), ("z", "C", 0, 1, 1, 1),
+        ("z", "D", 0, 1, 1, 1), ("z", "C", 0, 1, 1, 2), ("z", "C", 0, 0, 1, 0), ("z", "C", 0, 1, 0, 0), ("1", "A", 0, 1, 1),
+        ("1", "A", 0, 1, 2), ("1", "B", 0, 1, 1), ("z", "D", 0, 0, 1, 0), ("z", "D", 0, 1, 0, 0), ("z", "C", 0, 0, 1, 1),
+        ("z", "C", 0, 1, 0, 1), ("z", "D", 0, 0, 1, 1), ("z", "C", 0, 0, 0, 0), ("z", "D", 0, 0, 0, 0), ("1", "B", 0, 1, 2),
+        ("1", "B", 0, 0, 0), ("z", "D", 0, 1, 0, 1), ("z", "D", 0, 1, 1, 2), ("z", "C", 0, 0, 0, 1), ("z", "C", 0, 0, 1, 2),
+        ("z", "C", 0, 1, 0, 2), ("z", "D", 0, 0, 0, 1), ("z", "D", 0, 0, 1, 2), ("1", "A", 0, 0, 0), ("2", "B", 0, 0),
+        ("z", "D", 0, 1, 0, 2), ("z", "C", 0, 0, 0, 2), ("z", "D", 0, 0, 0, 2), ("2", "A", 0, 0), ("1", "A", 0, 0, 1),
+        ("2", "B", 0, 1), ("2", "A", 0, 1), ("1", "B", 0, 0, 1), ("3", "B", 0, 0), ("1", "A", 0, 0, 2), ("1", "A", 0, 1, 3),
+        ("2", "A", 0, 2), ("3", "A", 0, 0), ("1", "B", 0, 0, 2), ("3", "A", 0, 1), ("2", "B", 0, 2), ("x", "C", 0, 1),
+        ("1", "B", 0, 1, 3), ("3", "B", 0, 1), ("x", "D", 0, 1), ("3", "A", 0, 2), ("1", "A", 0, 0, 3), ("x", "C", 0, 0),
+        ("1", "B", 0, 0, 3), ("2", "A", 0, 3), ("3", "B", 0, 2), ("2", "B", 0, 3), ("y", "C", 0), ("y", "D", 0),
+        ("x", "D", 0, 0),
+    ),
+)
 
 
 def adamw_shard(grad, weight_now, moment_now, second_now):
@@ -358,6 +419,319 @@
     return tuple(array.reshape(weight.shape) for array in outs)
 
 
+AXES = {"A": (0, 1), "B": (1, 0), "C": (0, 1), "D": (1, 0)}
+
+
+def flipped(family, first, second):
+    return (first, second) if AXES[family][0] == 0 else (second, first)
+
+
+def planes_beside(z, planes):
+    return [p for p in (z - 1, z + 1) if 0 <= p < planes]
+
+
+def send_table(z, planes):
+    table = {}
+    for f, chunks in CHUNKS.items():
+        first, second = AXES[f]
+        for k in range(planes):
+            for c in range(len(chunks)):
+                if f in "AB":
+                    for b in range(2):
+                        table["1", f, c, b, k] = (first, z, (), flipped(f, 1, b) + (k,))
+                    table["2", f, c, k] = (second, z, (("1", f, c, 1, k),), flipped(f, 0, 1) + (k,))
+                    if k != z:
+                        table["3", f, c, k] = (2, k, (("1", f, c, 0, k), ("2", f, c, k)), (0, 0, k))
+                elif k != z:
+                    toward = 1 if k > z else -1
+                    for a in range(2):
+                        for b in range(2):
+                            before = z - toward
+                            needs = (("z", f, c, a, b, k, before),) if 0 <= before < planes else ()
+                            table["z", f, c, a, b, k] = (2, z + toward, needs, (a, b, k))
+                else:
+                    def crossed(place):
+                        return tuple(("z", f, c, *place, z, p) for p in planes_beside(z, planes))
+
+                    for b in range(2):
+                        place = flipped(f, 1, b)
+                        table["x", f, c, b] = (first, z, crossed(place), place + (z,))
+                    place = flipped(f, 0, 1)
+                    table["y", f, c] = (second, z, crossed(place) + (("x", f, c, 1),), place + (z,))
+    return table
+
+
+def last_needs(f, c, z, planes):
+    if f in "AB":
+        return [("1", f, c, 0, z), ("2", f, c, z)] + [("3", f, c, p) for p in range(planes) if p != z]
+    return [("z", f, c, 0, 0, z, p) for p in planes_beside(z, planes)] + [("x", f, c, 0), ("y", f, c)]
+
+
+def key_there(key, z):
+    return key[:-1] + (z,) if key[0] == "3" else key + (z,) if key[0] == "z" else key
+
+
+def spans_of(piece):
+    tiles = piece // 8
+    total = sum(sum(chunks) for chunks in CHUNKS.values())
+    spans, at = {}, 0
+    for f, chunks in CHUNKS.items():
+        for c, size in enumerate(chunks):
+            rows = size * tiles // total * 8
+            spans[f, c] = (at, rows)
+            at += rows
+    return spans
+
+
+def arrivals(z, planes, spans):
+    slots, at = {}, 0
+    for source in range(planes):
+        for key, (axis, target, needs, owner) in send_table(source, planes).items():
+            if target == z:
+                rows = spans[key[1], key[2]][1]
+                slots[key_there(key, source)] = (at, rows, len(slots))
+                at += rows
+    return slots, at
+
+
+def fast_kernel(digits, micro, acts, cotan, counts, weight, moment, second, packed, counts_held, acts_held, cotan_held,
+                acts_out, cotan_out, acts_in, cotan_in, rhs, grad, got, state, shard, load_sem, part_send, part_recv,
+                send_sem, recv_sem, up_sem):
+    section = lax.axis_index("section")
+    dp = lax.axis_index("dp")
+    mirror = (dp, lax.axis_size("section") - 1 - section)
+    planes = digits[2][0]
+    strides = [stride for count, stride in digits]
+    here = [lax.rem(lax.div(dp, stride), count) for count, stride in digits]
+    across = [(1 - 2 * here[axis]) * strides[axis] for axis in range(2)]
+    rows, depth = acts.shape[1], acts.shape[2]
+    width = cotan.shape[2]
+    slots = rows // micro
+    pieces = lax.axis_size("dp")
+    piece = depth // pieces
+    per_row = width // LANES
+    spans = spans_of(piece)
+    tables = [send_table(z, planes) for z in range(planes)]
+    landings = [arrivals(z, planes, spans)[0] for z in range(planes)]
+
+    loads = [
+        pltpu.make_async_copy(cotan, cotan_held, load_sem.at[0]),
+        pltpu.make_async_copy(counts, counts_held, load_sem.at[1]),
+        pltpu.make_async_copy(acts.at[1], acts_held.at[1], load_sem.at[2]),
+        pltpu.make_async_copy(acts.at[0], acts_held.at[0], load_sem.at[3]),
+    ]
+    loads += [pltpu.make_async_copy(array, state.at[i], load_sem.at[4 + i]) for i, array in enumerate((weight, moment, second))]
+    for load in loads[:4]:
+        load.start()
+
+    barrier = pltpu.get_barrier_semaphore()
+    pl.semaphore_signal(barrier, inc=1, device_id=mirror, device_id_type=MESH)
+    for axis in range(2):
+        @pl.when(here[axis] == 0)
+        def greet():
+            pl.semaphore_signal(barrier, inc=1, device_id=(dp + across[axis], section), device_id_type=MESH)
+    for step in range(1, planes):
+        @pl.when(here[2] + step < planes)
+        def greet_plane():
+            pl.semaphore_signal(barrier, inc=1, device_id=(dp + step * strides[2], section), device_id_type=MESH)
+
+    def masked(k):
+        parts = []
+        for b in range(micro):
+            block = cotan_held[k, b * slots:(b + 1) * slots, :].astype(jnp.float32)
+            place = lax.broadcasted_iota(jnp.int32, (slots, width), 0)
+            parts.append(jnp.where(place < counts_held[b, k], block, 0.0))
+        return parts[0] if micro == 1 else jnp.concatenate(parts, axis=0)
+
+    def to_mirror(src, dst, at):
+        return pltpu.make_async_remote_copy(
+            src_ref=src, dst_ref=dst, send_sem=part_send.at[at], recv_sem=part_recv.at[at],
+            device_id=mirror, device_id_type=MESH)
+
+    exchange = [to_mirror(acts_out.at[at], acts_in.at[at], at) for at in range(pieces)]
+    exchange.append(to_mirror(cotan_out, cotan_in, pieces))
+    loads[0].wait()
+    loads[1].wait()
+    cotan_out[...] = masked(1)
+    pl.semaphore_wait(barrier, 1 + here[0] + here[1] + here[2])
+    exchange[pieces].start()
+    rhs[0:rows, :] = masked(0).astype(jnp.bfloat16)
+    for axis in range(2):
+        @pl.when(here[axis] == 1)
+        def answer():
+            pl.semaphore_signal(up_sem.at[axis], inc=1, device_id=(dp + across[axis], section), device_id_type=MESH)
+    for step in range(1, planes):
+        @pl.when(here[2] >= step)
+        def answer_plane():
+            pl.semaphore_signal(up_sem.at[1 + step], inc=1, device_id=(dp - step * strides[2], section), device_id_type=MESH)
+    loads[2].wait()
+
+    def run(z):
+        table, landing = tables[z], landings[z]
+        order = ORDERS[z]
+        owners = []
+        for key in order:
+            if table[key][3] not in owners:
+                owners.append(table[key][3])
+        owners.append((0, 0, z))
+
+        def owner_index(owner):
+            return dp + owner[0] * across[0] + owner[1] * across[1] + (owner[2] - z) * strides[2]
+
+        def columns(owner):
+            return pl.ds(pl.multiple_of(owner_index(owner) * piece, LANES), piece)
+
+        for at, owner in enumerate(owners):
+            acts_out[at] = acts_held[1, :, columns(owner)].astype(jnp.float32)
+            exchange[at].start()
+        for load in loads[4:]:
+            load.start()
+        loads[3].wait()
+        exchange[pieces].wait_recv()
+        rhs[rows:2 * rows, :] = cotan_in[...].astype(jnp.bfloat16)
+
+        def make(at):
+            exchange[at].wait_recv()
+            lhs = jnp.concatenate([acts_held[0, :, columns(owners[at])], acts_in[at].astype(jnp.bfloat16)], axis=0)
+            first = pl.multiple_of(owner_index(owners[at]) * piece, piece)
+            grad[pl.ds(first, piece), :] = lax.dot_general(
+                lhs, rhs[...], (((0,), (0,)), ((), ())), preferred_element_type=jnp.float32)
+
+        def block(owner, span):
+            return pl.ds(pl.multiple_of(owner_index(owner) * piece + span[0], 8), span[1])
+
+        def copy_of(key):
+            axis, target, needs, owner = table[key]
+            place, size, at = landings[target][key_there(key, z)]
+            device = dp + across[axis] if axis < 2 else dp + (target - z) * strides[2]
+            return pltpu.make_async_remote_copy(
+                src_ref=grad.at[block(owner, spans[key[1], key[2]]), :], dst_ref=got.at[pl.ds(place, size), :],
+                send_sem=send_sem.at[sends.index(key)], recv_sem=recv_sem.at[at],
+                device_id=(device, section), device_id_type=MESH)
+
+        def arrived(key):
+            place, size, at = landing[key]
+            pltpu.make_async_remote_copy(
+                src_ref=grad.at[pl.ds(0, size), :], dst_ref=got.at[pl.ds(place, size), :],
+                send_sem=send_sem.at[0], recv_sem=recv_sem.at[at],
+                device_id=mirror, device_id_type=MESH).wait_recv()
+            return got[place:place + size, :]
+
+        sends = list(order)
+        met, done = set(), 0
+        for key in order:
+            axis, target, needs, owner = table[key]
+            while done <= owners.index(owner):
+                make(done)
+                done += 1
+            if needs:
+                at = block(owner, spans[key[1], key[2]])
+                total = grad[at, :]
+                for need in needs:
+                    total += arrived(need)
+                grad[at, :] = total
+            if axis < 2 and axis not in met:
+                met.add(axis)
+
+                @pl.when(here[axis] == 0)
+                def wait_up():
+                    pl.semaphore_wait(up_sem.at[axis], 1)
+            if axis == 2 and target > z and 1 + target - z not in met:
+                met.add(1 + target - z)
+                pl.semaphore_wait(up_sem.at[1 + target - z], 1)
+            copy_of(key).start()
+        while done < pieces:
+            make(done)
+            done += 1
+        for load in loads[4:]:
+            load.wait()
+        for f, c in FINALS:
+            span = spans[f, c]
+            total = grad[block((0, 0, z), span), :]
+            for need in last_needs(f, c, z, planes):
+                total += arrived(need)
+            for part in range(per_row):
+                shard[pl.ds(span[0] * per_row + part, span[1], stride=per_row), :] = total[:, part * LANES:(part + 1) * LANES]
+            flat = slice(span[0] * per_row, (span[0] + span[1]) * per_row)
+            updated = adamw_shard(shard[flat, :], state[0, flat, :], state[1, flat, :], state[2, flat, :])
+            for i in range(3):
+                packed[i, flat, :] = updated[i]
+        for copy in exchange:
+            copy.wait_send()
+        for key in sends:
+            copy_of(key).wait_send()
+
+    for z in range(planes):
+        pl.when(here[2] == z)(functools.partial(run, z))
+
+
+def put_kernel(packed, new_weight, new_moment, new_second, sem):
+    copies = [pltpu.make_async_copy(packed.at[i], out, sem.at[i]) for i, out in enumerate((new_weight, new_moment, new_second))]
+    for copy in copies:
+        copy.start()
+    for copy in copies:
+        copy.wait()
+
+
+def fast_fits(digits, acts, cotan, weight):
+    planes, depth, width = digits[2][0], acts.shape[3], cotan.shape[3]
+    piece = depth // (4 * planes)
+    total = sum(sum(chunks) for chunks in CHUNKS.values())
+    return (digits[0][0] == 2 and digits[1][0] == 2 and planes == len(ORDERS) and piece % LANES == 0 and piece % (8 * total) == 0
+            and width % LANES == 0 and piece * width == weight.shape[1])
+
+
+def fast_shards(digits, acts, cotan, counts, weight, moment, second):
+    micro = counts.shape[3]
+    rows, depth = acts.shape[2], acts.shape[3]
+    width = cotan.shape[3]
+    shard_rows = weight.shape[1] // LANES
+    planes = digits[2][0]
+    pieces = 4 * planes
+    spans = spans_of(depth // pieces)
+    landings = [arrivals(z, planes, spans) for z in range(planes)]
+    received = max(len(slots) for slots, total in landings)
+    space = max(total for slots, total in landings)
+    sent = max(len(send_table(z, planes)) for z in range(planes))
+    hbm = pl.BlockSpec(memory_space=pl.ANY)
+    vmem = pl.BlockSpec(memory_space=pltpu.VMEM)
+    flat = (shard_rows, LANES)
+    packed = pl.pallas_call(
+        functools.partial(fast_kernel, digits, micro),
+        out_shape=pltpu.VMEM((3, *flat), jnp.float32),
+        in_specs=[hbm] * 6,
+        out_specs=vmem,
+        scratch_shapes=[
+            pltpu.SMEM((micro, 2), jnp.int32),
+            pltpu.VMEM((2, rows, depth), jnp.bfloat16),
+            pltpu.VMEM((2, rows, width), jnp.bfloat16),
+            pltpu.VMEM((pieces, rows, depth // pieces), jnp.float32),
+            pltpu.VMEM((rows, width), jnp.float32),
+            pltpu.VMEM((pieces, rows, depth // pieces), jnp.float32),
+            pltpu.VMEM((rows, width), jnp.float32),
+            pltpu.VMEM((2 * rows, width), jnp.bfloat16),
+            pltpu.VMEM((depth, width), jnp.float32),
+            pltpu.VMEM((space, width), jnp.float32),
+            pltpu.VMEM((3, *flat), jnp.float32),
+            pltpu.VMEM(flat, jnp.float32),
+            pltpu.SemaphoreType.DMA((7,)), pltpu.SemaphoreType.DMA((pieces + 1,)), pltpu.SemaphoreType.DMA((pieces + 1,)),
+            pltpu.SemaphoreType.DMA((sent,)), pltpu.SemaphoreType.DMA((received,)),
+            pltpu.SemaphoreType.REGULAR((1 + planes,)),
+        ],
+        compiler_params=pltpu.CompilerParams(collective_id=0, has_side_effects=True, vmem_limit_bytes=66 * 10**6),
+        name="reduce_adamw",
+    )(acts[0], cotan[0], counts[0, :, 0, :].T, *(array.reshape(flat) for array in (weight, moment, second)))
+    outs = pl.pallas_call(
+        put_kernel,
+        out_shape=(jax.ShapeDtypeStruct(flat, jnp.float32),) * 3,
+        in_specs=[vmem],
+        out_specs=(hbm, hbm, hbm),
+        scratch_shapes=[pltpu.SemaphoreType.DMA((3,))],
+        name="put",
+    )(pltpu.with_memory_space_constraint(packed, pltpu.VMEM))
+    return tuple(array.reshape(weight.shape) for array in outs)
+
+
 def solution(mesh):
     in_specs = (
         P("section", None, "dp", None),
@@ -368,5 +742,10 @@
         P("section", "dp"),
     )
     out_specs = (P("section", "dp"), P("section", "dp"), P("section", "dp"))
-    body = functools.partial(shards, dp_digits(mesh))
+    digits = dp_digits(mesh)
+
+    def body(acts, cotan, counts, weight, moment, second):
+        form = fast_shards if fast_fits(digits, acts, cotan, weight) else shards
+        return form(digits, acts, cotan, counts, weight, moment, second)
+
     return jax.shard_map(body, mesh=mesh, in_specs=in_specs, out_specs=out_specs, check_vma=False)

time: 38.8 us -> 33.3 us (0.86)
  Pallas kernels: 38 us -> 32.4 us
    pallas_call x2, Pallas kernels: 37.9 us -> 32.4 us  [the longest x1 31.5 us: fast_shards(): pl.pallas_call(functools.partial(fast_kernel, digits, micro), out_shape=p...]
where the time goes in v1:
time: 33.3 us; the launch traced here: 33 us
  Pallas kernels  32.4 us (97%)
  between operations  0.64 us (2%)
    pallas_call x1, Pallas kernels, fast_shards(): pl.pallas_call(functools.partial(fast_kernel, digits, micro), out_shape=p...  31.5 us
    pallas_call x1, Pallas kernels, fast_shards(): pl.pallas_call(put_kernel, out_shape=(jax.ShapeDtypeStruct(flat, jnp.floa...  0.83 us

profile of v1, /device:TPU:0, one launch (start us, length us, event | category | flops | bytes accessed | tf_op | source)
XLA Modules:
  0.0 33.0 jit_solution(13232008767065684881)
XLA Ops:
  0.6 31.5 %reduce_adamw.1.packed = f32[3,384,128]{2,1,0:T(8,128)S(1)} custom-call(bf16[2,128,2048]{2,1,0:T(8,128)(2,1)} %bitcast.9, bf16[2,128,384]{2,1,0:T(8,128)(2,1)} %bitcast.10, s32[1,2]{1,0:T(1,128)} %bitcast.14, f32[384,128]{1,0:T(8,128)} %bitcast.11, f32[384,128]{1,0:T(8,128)} %bitcast.12, f32[384,128]{1,0:T(8,128)} %bitcast.13), custom_call_target="tpu_custom_call" | custom-call | tf_op jit(solution)/shard_map/reduce_adamw/pallas_call | solution.py:699
  32.2 0.8 %put.1 = (f32[384,128]{1,0:T(8,128)}, f32[384,128]{1,0:T(8,128)}, f32[384,128]{1,0:T(8,128)}) custom-call(f32[3,384,128]{2,1,0:T(8,128)S(1)} %reduce_adamw.1.packed), custom_call_target="tpu_custom_call" | custom-call | tf_op jit(solution)/shard_map/put/pallas_call | solution.py:724

commit v2 on v1

--- a/solution.py
+++ b/solution.py
@@ -10,63 +10,56 @@
 MESH = pl.DeviceIdType.MESH
 
 
-CHUNKS = {"A": (7,), "B": (7,), "C": (1,), "D": (1,)}
-FINALS = (("C", 0), ("D", 0), ("A", 0), ("B", 0))
+CHUNKS = {"A": (7,), "B": (6,), "Z": ((1, 2),)}
+LASTS = (
+    (("C", 0), ("D", 0), ("A", 0), ("B", 0)),
+    (("C", 0), ("D", 0), ("A", 0), ("B", 0)),
+    (("C", 0), ("D", 0), ("A", 0), ("B", 0)),
+    (("C", 0), ("D", 0), ("A", 0), ("B", 0)),
+)
 ORDERS = (
     (
-        ("1", "A", 0, 1, 3), ("1", "B", 0, 1, 3), ("z", "C", 0, 1, 1, 3), ("z", "D", 0, 1, 1, 3), ("z", "C", 0, 1, 1, 2),
-        ("z", "D", 0, 1, 1, 2), ("z", "C", 0, 1, 1, 1), ("z", "C", 0, 0, 1, 3), ("z", "C", 0, 1, 0, 3), ("1", "A", 0, 1, 2),
-        ("1", "A", 0, 1, 1), ("1", "B", 0, 1, 2), ("z", "D", 0, 0, 1, 3), ("z", "D", 0, 1, 0, 3), ("z", "C", 0, 0, 1, 2),
-        ("z", "C", 0, 1, 0, 2), ("z", "D", 0, 1, 1, 1), ("z", "C", 0, 0, 0, 3), ("z", "D", 0, 0, 1, 2), ("1", "B", 0, 1, 1),
-        ("1", "B", 0, 0, 3), ("z", "D", 0, 1, 0, 2), ("z", "D", 0, 0, 0, 3), ("z", "C", 0, 0, 1, 1), ("z", "C", 0, 1, 0, 1),
-        ("z", "C", 0, 0, 0, 2), ("z", "D", 0, 0, 1, 1), ("z", "D", 0, 1, 0, 1), ("1", "A", 0, 0, 3), ("2", "B", 0, 3),
-        ("z", "D", 0, 0, 0, 2), ("z", "C", 0, 0, 0, 1), ("z", "D", 0, 0, 0, 1), ("2", "A", 0, 3), ("1", "A", 0, 0, 2),
-        ("2", "B", 0, 2), ("2", "A", 0, 2), ("1", "B", 0, 0, 2), ("3", "B", 0, 3), ("1", "A", 0, 1, 0), ("1", "A", 0, 0, 1),
-        ("2", "A", 0, 1), ("3", "A", 0, 3), ("1", "B", 0, 1, 0), ("3", "A", 0, 2), ("2", "B", 0, 1), ("x", "C", 0, 1),
-        ("1", "B", 0, 0, 1), ("3", "B", 0, 2), ("x", "D", 0, 1), ("1", "A", 0, 0, 0), ("x", "C", 0, 0), ("2", "A", 0, 0),
-        ("3", "A", 0, 1), ("1", "B", 0, 0, 0), ("2", "B", 0, 0), ("3", "B", 0, 1), ("y", "C", 0), ("y", "D", 0),
-        ("x", "D", 0, 0),
+        ("1", "A", 0, 1, 2), ("z", 0, 0, 1, 3), ("1", "B", 0, 1, 1), ("z", 0, 1, 0, 3), ("z", 0, 1, 1, 3), ("z", 0, 0, 0, 3),
+        ("1", "A", 0, 1, 3), ("z", 0, 1, 1, 2), ("z", 0, 1, 0, 2), ("1", "B", 0, 1, 0), ("z", 0, 0, 0, 2), ("1", "A", 0, 0, 3),
+        ("z", 0, 1, 1, 1), ("2", "A", 0, 2), ("1", "A", 0, 1, 0), ("1", "A", 0, 1, 1), ("z", 0, 0, 1, 2), ("2", "A", 0, 3),
+        ("1", "B", 0, 1, 3), ("z", 0, 0, 1, 1), ("1", "B", 0, 1, 2), ("z", 0, 1, 0, 1), ("1", "B", 0, 0, 3), ("z", 0, 0, 0, 1),
+        ("1", "A", 0, 0, 2), ("1", "B", 0, 0, 1), ("2", "B", 0, 1), ("3", "A", 0, 3), ("2", "B", 0, 3), ("x", "D", 0, 1),
+        ("1", "B", 0, 0, 2), ("x", "C", 0, 1), ("2", "B", 0, 2), ("1", "A", 0, 0, 1), ("2", "A", 0, 1), ("3", "A", 0, 2),
+        ("2", "B", 0, 0), ("2", "A", 0, 0), ("3", "B", 0, 3), ("1", "A", 0, 0, 0), ("3", "B", 0, 1), ("y", "D", 0),
+        ("1", "B", 0, 0, 0), ("x", "C", 0, 0), ("3", "B", 0, 2), ("3", "A", 0, 1), ("x", "D", 0, 0), ("y", "C", 0),
     ),
     (
-        ("1", "A", 0, 1, 3), ("1", "B", 0, 1, 3), ("1", "A", 0, 1, 0), ("1", "A", 0, 1, 2), ("1", "B", 0, 1, 0),
-        ("z", "C", 0, 1, 1, 3), ("z", "D", 0, 1, 1, 3), ("z", "C", 0, 1, 1, 2), ("z", "D", 0, 1, 1, 2), ("1", "B", 0, 1, 2),
-        ("z", "C", 0, 0, 1, 3), ("z", "C", 0, 1, 0, 3), ("z", "D", 0, 0, 1, 3), ("z", "D", 0, 1, 0, 3), ("z", "C", 0, 0, 1, 2),
-        ("z", "C", 0, 1, 0, 2), ("1", "A", 0, 0, 3), ("2", "B", 0, 3), ("2", "A", 0, 3), ("z", "C", 0, 0, 0, 3),
-        ("z", "D", 0, 0, 1, 2), ("z", "D", 0, 1, 0, 2), ("z", "D", 0, 0, 0, 3), ("z", "C", 0, 0, 0, 2), ("1", "B", 0, 0, 3),
-        ("z", "D", 0, 0, 0, 2), ("z", "C", 0, 1, 1, 0), ("z", "D", 0, 1, 1, 0), ("1", "A", 0, 0, 0), ("1", "A", 0, 1, 1),
-        ("2", "A", 0, 0), ("z", "C", 0, 0, 1, 0), ("z", "C", 0, 1, 0, 0), ("z", "D", 0, 0, 1, 0), ("z", "D", 0, 1, 0, 0),
-        ("3", "A", 0, 3), ("2", "A", 0, 2), ("z", "C", 0, 0, 0, 0), ("z", "D", 0, 0, 0, 0), ("1", "A", 0, 0, 2),
-        ("2", "B", 0, 0), ("1", "B", 0, 0, 0), ("1", "B", 0, 1, 1), ("2", "B", 0, 2), ("x", "C", 0, 1), ("1", "B", 0, 0, 2),
-        ("x", "D", 0, 1), ("1", "A", 0, 0, 1), ("x", "C", 0, 0), ("2", "A", 0, 1), ("3", "A", 0, 0), ("3", "B", 0, 3),
-        ("1", "B", 0, 0, 1), ("2", "B", 0, 1), ("3", "B", 0, 0), ("3", "A", 0, 2), ("y", "C", 0), ("y", "D", 0),
-        ("x", "D", 0, 0), ("3", "B", 0, 2),
+        ("1", "A", 0, 1, 3), ("1", "B", 0, 1, 3), ("1", "A", 0, 1, 2), ("1", "B", 0, 1, 0), ("z", 0, 0, 1, 3),
+        ("1", "A", 0, 1, 0), ("1", "B", 0, 1, 2), ("z", 0, 1, 1, 3), ("1", "A", 0, 0, 3), ("2", "A", 0, 3),
+        ("1", "B", 0, 0, 1), ("z", 0, 1, 0, 3), ("1", "B", 0, 0, 3), ("z", 0, 1, 1, 2), ("1", "A", 0, 0, 2), ("z", 0, 0, 0, 3),
+        ("2", "A", 0, 2), ("1", "B", 0, 1, 1), ("2", "B", 0, 3), ("z", 0, 1, 0, 2), ("2", "A", 0, 0), ("z", 0, 0, 0, 2),
+        ("x", "C", 0, 1), ("z", 0, 1, 1, 0), ("z", 0, 0, 1, 2), ("z", 0, 0, 0, 0), ("1", "A", 0, 0, 0), ("3", "A", 0, 3),
+        ("2", "B", 0, 2), ("z", 0, 0, 1, 0), ("x", "D", 0, 1), ("2", "B", 0, 0), ("3", "B", 0, 3), ("z", 0, 1, 0, 0),
+        ("1", "A", 0, 0, 1), ("3", "A", 0, 2), ("1", "B", 0, 0, 0), ("1", "B", 0, 0, 2), ("3", "A", 0, 0), ("1", "A", 0, 1, 1),
+        ("y", "C", 0), ("y", "D", 0), ("2", "B", 0, 1), ("x", "D", 0, 0), ("3", "B", 0, 0), ("3", "B", 0, 2), ("2", "A", 0, 1),
+        ("x", "C", 0, 0),
     ),
     (
-        ("1", "A", 0, 1, 0), ("1", "B", 0, 1, 0), ("1", "A", 0, 1, 1), ("1", "A", 0, 1, 3), ("1", "B", 0, 1, 1),
-        ("1", "B", 0, 1, 3), ("z", "C", 0, 1, 1, 3), ("z", "C", 0, 1, 1, 0), ("z", "D", 0, 1, 1, 3), ("z", "D", 0, 1, 1, 0),
-        ("z", "C", 0, 1, 1, 1), ("z", "D", 0, 1, 1, 1), ("1", "A", 0, 0, 0), ("2", "B", 0, 0), ("2", "A", 0, 0),
-        ("z", "C", 0, 0, 1, 3), ("z", "C", 0, 0, 1, 0), ("z", "C", 0, 1, 0, 3), ("z", "C", 0, 1, 0, 0), ("z", "D", 0, 0, 1, 3),
-        ("z", "D", 0, 0, 1, 0), ("z", "D", 0, 1, 0, 3), ("z", "D", 0, 1, 0, 0), ("z", "C", 0, 0, 1, 1), ("z", "C", 0, 1, 0, 1),
-        ("1", "B", 0, 0, 0), ("z", "D", 0, 0, 1, 1), ("z", "C", 0, 0, 0, 3), ("z", "C", 0, 0, 0, 0), ("z", "D", 0, 0, 0, 0),
-        ("z", "D", 0, 1, 0, 1), ("z", "D", 0, 0, 0, 3), ("z", "C", 0, 0, 0, 1), ("1", "A", 0, 0, 1), ("1", "A", 0, 1, 2),
-        ("2", "A", 0, 1), ("z", "D", 0, 0, 0, 1), ("3", "A", 0, 0), ("2", "A", 0, 3), ("3", "B", 0, 0), ("1", "A", 0, 0, 3),
-        ("2", "B", 0, 1), ("1", "B", 0, 0, 1), ("1", "B", 0, 1, 2), ("2", "B", 0, 3), ("x", "C", 0, 1), ("1", "B", 0, 0, 3),
-        ("3", "A", 0, 3), ("x", "D", 0, 1), ("1", "A", 0, 0, 2), ("x", "C", 0, 0), ("2", "A", 0, 2), ("1", "B", 0, 0, 2),
-        ("2", "B", 0, 2), ("3", "A", 0, 1), ("3", "B", 0, 3), ("y", "C", 0), ("y", "D", 0), ("x", "D", 0, 0), ("3", "B", 0, 1),
+        ("1", "A", 0, 1, 0), ("1", "B", 0, 1, 0), ("1", "A", 0, 0, 0), ("1", "A", 0, 1, 1), ("1", "A", 0, 1, 3),
+        ("1", "B", 0, 1, 1), ("1", "B", 0, 0, 0), ("z", 0, 1, 1, 1), ("2", "A", 0, 0), ("2", "B", 0, 0), ("z", 0, 1, 1, 0),
+        ("1", "A", 0, 1, 2), ("z", 0, 0, 0, 0), ("z", 0, 0, 1, 3), ("z", 0, 0, 1, 1), ("1", "A", 0, 0, 3), ("z", 0, 0, 1, 0),
+        ("1", "B", 0, 1, 3), ("z", 0, 1, 0, 0), ("1", "B", 0, 0, 1), ("z", 0, 1, 0, 3), ("z", 0, 1, 0, 1), ("2", "B", 0, 1),
+        ("3", "A", 0, 0), ("1", "B", 0, 0, 3), ("x", "C", 0, 1), ("z", 0, 0, 0, 1), ("2", "A", 0, 3), ("z", 0, 0, 0, 3),
+        ("x", "D", 0, 1), ("1", "A", 0, 0, 1), ("2", "A", 0, 1), ("2", "B", 0, 3), ("1", "B", 0, 1, 2), ("2", "A", 0, 2),
+        ("z", 0, 1, 1, 3), ("3", "B", 0, 0), ("3", "A", 0, 3), ("x", "D", 0, 0), ("1", "A", 0, 0, 2), ("3", "B", 0, 1),
+        ("x", "C", 0, 0), ("y", "D", 0), ("1", "B", 0, 0, 2), ("3", "B", 0, 3), ("3", "A", 0, 1), ("2", "B", 0, 2),
+        ("y", "C", 0),
     ),
     (
-        ("1", "A", 0, 1, 0), ("1", "B", 0, 1, 0), ("z", "C", 0, 1, 1, 0), ("z", "D", 0, 1, 1, 0), ("z", "C", 0, 1, 1, 1),
-        ("z", "D", 0, 1, 1, 1), ("z", "C", 0, 1, 1, 2), ("z", "C", 0, 0, 1, 0), ("z", "C", 0, 1, 0, 0), ("1", "A", 0, 1, 1),
-        ("1", "A", 0, 1, 2), ("1", "B", 0, 1, 1), ("z", "D", 0, 0, 1, 0), ("z", "D", 0, 1, 0, 0), ("z", "C", 0, 0, 1, 1),
-        ("z", "C", 0, 1, 0, 1), ("z", "D", 0, 0, 1, 1), ("z", "C", 0, 0, 0, 0), ("z", "D", 0, 0, 0, 0), ("1", "B", 0, 1, 2),
-        ("1", "B", 0, 0, 0), ("z", "D", 0, 1, 0, 1), ("z", "D", 0, 1, 1, 2), ("z", "C", 0, 0, 0, 1), ("z", "C", 0, 0, 1, 2),
-        ("z", "C", 0, 1, 0, 2), ("z", "D", 0, 0, 0, 1), ("z", "D", 0, 0, 1, 2), ("1", "A", 0, 0, 0), ("2", "B", 0, 0),
-        ("z", "D", 0, 1, 0, 2), ("z", "C", 0, 0, 0, 2), ("z", "D", 0, 0, 0, 2), ("2", "A", 0, 0), ("1", "A", 0, 0, 1),
-        ("2", "B", 0, 1), ("2", "A", 0, 1), ("1", "B", 0, 0, 1), ("3", "B", 0, 0), ("1", "A", 0, 0, 2), ("1", "A", 0, 1, 3),
-        ("2", "A", 0, 2), ("3", "A", 0, 0), ("1", "B", 0, 0, 2), ("3", "A", 0, 1), ("2", "B", 0, 2), ("x", "C", 0, 1),
-        ("1", "B", 0, 1, 3), ("3", "B", 0, 1), ("x", "D", 0, 1), ("3", "A", 0, 2), ("1", "A", 0, 0, 3), ("x", "C", 0, 0),
-        ("1", "B", 0, 0, 3), ("2", "A", 0, 3), ("3", "B", 0, 2), ("2", "B", 0, 3), ("y", "C", 0), ("y", "D", 0),
-        ("x", "D", 0, 0),
+        ("z", 0, 1, 1, 1), ("1", "A", 0, 1, 0), ("1", "B", 0, 1, 0), ("1", "A", 0, 0, 0), ("1", "A", 0, 1, 1),
+        ("1", "B", 0, 1, 1), ("z", 0, 1, 1, 0), ("z", 0, 0, 0, 0), ("z", 0, 0, 1, 1), ("z", 0, 0, 1, 0), ("z", 0, 1, 0, 0),
+        ("1", "B", 0, 1, 2), ("z", 0, 1, 0, 1), ("z", 0, 0, 0, 1), ("2", "B", 0, 0), ("1", "A", 0, 1, 2), ("z", 0, 1, 1, 2),
+        ("1", "B", 0, 0, 0), ("1", "A", 0, 0, 1), ("2", "A", 0, 0), ("z", 0, 0, 1, 2), ("1", "B", 0, 0, 2), ("2", "A", 0, 1),
+        ("2", "B", 0, 2), ("1", "B", 0, 0, 1), ("3", "B", 0, 0), ("1", "A", 0, 1, 3), ("z", 0, 0, 0, 2), ("1", "B", 0, 1, 3),
+        ("3", "A", 0, 0), ("2", "B", 0, 1), ("1", "A", 0, 0, 2), ("2", "A", 0, 2), ("x", "D", 0, 0), ("z", 0, 1, 0, 2),
+        ("3", "A", 0, 1), ("x", "D", 0, 1), ("1", "B", 0, 0, 3), ("x", "C", 0, 1), ("3", "B", 0, 2), ("x", "C", 0, 0),
+        ("1", "A", 0, 0, 3), ("3", "B", 0, 1), ("2", "A", 0, 3), ("2", "B", 0, 3), ("3", "A", 0, 2), ("y", "D", 0),
+        ("y", "C", 0),
     ),
 )
 
@@ -430,68 +423,109 @@
     return [p for p in (z - 1, z + 1) if 0 <= p < planes]
 
 
-def send_table(z, planes):
+def crossed(c, place, z, planes):
+    return tuple(("z", c, *place, z, p) for p in planes_beside(z, planes))
+
+
+def send_table(z, planes, spans):
     table = {}
-    for f, chunks in CHUNKS.items():
-        first, second = AXES[f]
-        for k in range(planes):
-            for c in range(len(chunks)):
-                if f in "AB":
+    for f, c in spans:
+        if f in AXES:
+            first, second = AXES[f]
+        if f in "AB":
+            for k in range(planes):
+                for b in range(2):
+                    table["1", f, c, b, k] = (first, z, (), flipped(f, 1, b) + (k,))
+                table["2", f, c, k] = (second, z, (("1", f, c, 1, k),), flipped(f, 0, 1) + (k,))
+                if k != z:
+                    table["3", f, c, k] = (2, k, (("1", f, c, 0, k), ("2", f, c, k)), (0, 0, k))
+        elif f in "CD":
+            for b in range(2):
+                place = flipped(f, 1, b)
+                table["x", f, c, b] = (first, z, crossed(c, place, z, planes), place + (z,))
+            place = flipped(f, 0, 1)
+            table["y", f, c] = (second, z, crossed(c, place, z, planes) + (("x", f, c, 1),), place + (z,))
+        else:
+            for k in range(planes):
+                toward = 1 if k > z else -1
+                for a in range(2 if k != z else 0):
                     for b in range(2):
-                        table["1", f, c, b, k] = (first, z, (), flipped(f, 1, b) + (k,))
-                    table["2", f, c, k] = (second, z, (("1", f, c, 1, k),), flipped(f, 0, 1) + (k,))
-                    if k != z:
-                        table["3", f, c, k] = (2, k, (("1", f, c, 0, k), ("2", f, c, k)), (0, 0, k))
-                elif k != z:
-                    toward = 1 if k > z else -1
-                    for a in range(2):
-                        for b in range(2):
-                            before = z - toward
-                            needs = (("z", f, c, a, b, k, before),) if 0 <= before < planes else ()
-                            table["z", f, c, a, b, k] = (2, z + toward, needs, (a, b, k))
-                else:
-                    def crossed(place):
-                        return tuple(("z", f, c, *place, z, p) for p in planes_beside(z, planes))
-
-                    for b in range(2):
-                        place = flipped(f, 1, b)
-                        table["x", f, c, b] = (first, z, crossed(place), place + (z,))
-                    place = flipped(f, 0, 1)
-                    table["y", f, c] = (second, z, crossed(place) + (("x", f, c, 1),), place + (z,))
+                        needs = (("z", c, a, b, k, z - toward),) if 0 <= z - toward < planes else ()
+                        table["z", c, a, b, k] = (2, z + toward, needs, (a, b, k))
     return table
 
 
 def last_needs(f, c, z, planes):
     if f in "AB":
-        return [("1", f, c, 0, z), ("2", f, c, z)] + [("3", f, c, p) for p in range(planes) if p != z]
-    return [("z", f, c, 0, 0, z, p) for p in planes_beside(z, planes)] + [("x", f, c, 0), ("y", f, c)]
+        return (("1", f, c, 0, z), ("2", f, c, z)) + tuple(("3", f, c, p) for p in range(planes) if p != z)
+    return crossed(c, (0, 0), z, planes) + (("x", f, c, 0), ("y", f, c))
+
+
+def wait_groups(z, planes, spans):
+    groups = []
+    for f, c in spans:
+        if f in "AB":
+            for k in range(planes):
+                groups.append((("1", f, c, 1, k),))
+                groups.append((("1", f, c, 0, k), ("2", f, c, k)) if k != z else last_needs(f, c, z, planes))
+        elif f in "CD":
+            groups += [(("x", f, c, 1),), (("x", f, c, 0), ("y", f, c))]
+        else:
+            for place in ((0, 0), (0, 1), (1, 0), (1, 1)):
+                groups.append(crossed(c, place, z, planes))
+                for k in range(planes):
+                    before = z - 1 if k > z else z + 1
+                    if k != z and 0 <= before < planes:
+                        groups.append((("z", c, *place, k, before),))
+    return groups
 
 
 def key_there(key, z):
     return key[:-1] + (z,) if key[0] == "3" else key + (z,) if key[0] == "z" else key
 
 
+def span_of(key, spans):
+    return spans[("Z",) + key[1:2]] if key[0] == "z" else spans[key[1], key[2]]
+
+
 def spans_of(piece):
-    tiles = piece // 8
-    total = sum(sum(chunks) for chunks in CHUNKS.values())
+    total = sum(CHUNKS["A"]) + sum(CHUNKS["B"]) + sum(sum(pair) for pair in CHUNKS["Z"])
+    unit = piece // 8 // total * 8
     spans, at = {}, 0
-    for f, chunks in CHUNKS.items():
-        for c, size in enumerate(chunks):
-            rows = size * tiles // total * 8
-            spans[f, c] = (at, rows)
+    for f in "AB":
+        for c, size in enumerate(CHUNKS[f]):
+            spans[f, c] = (at, size * unit)
+            at += size * unit
+    for c, (first, second) in enumerate(CHUNKS["Z"]):
+        spans["Z", c] = (at, (first + second) * unit)
+        if first:
+            spans["C", c] = (at, first * unit)
+        if second:
+            spans["D", c] = (at + first * unit, second * unit)
+        at += (first + second) * unit
+    return spans
+
+
+def landing_of(z, planes, spans):
+    places, at, groups = {}, 0, wait_groups(z, planes, spans)
+    for i, group in enumerate(groups):
+        for key in group:
+            rows = span_of(key, spans)[1]
+            places[key] = (at, rows, i)
             at += rows
-    return spans
-
-
-def arrivals(z, planes, spans):
-    slots, at = {}, 0
-    for source in range(planes):
-        for key, (axis, target, needs, owner) in send_table(source, planes).items():
-            if target == z:
-                rows = spans[key[1], key[2]][1]
-                slots[key_there(key, source)] = (at, rows, len(slots))
-                at += rows
-    return slots, at
+    return places, groups, at
+
+
+def part_groups(pieces):
+    groups, at = [], 0
+    for size in (1, 1, 1, 1, 2, 2):
+        if at + size <= pieces:
+            groups.append((at, size))
+            at += size
+    while at < pieces:
+        groups.append((at, min(4, pieces - at)))
+        at += groups[-1][1]
+    return groups
 
 
 def fast_kernel(digits, micro, acts, cotan, counts, weight, moment, second, packed, counts_held, acts_held, cotan_held,
@@ -511,8 +545,9 @@
     piece = depth // pieces
     per_row = width // LANES
     spans = spans_of(piece)
-    tables = [send_table(z, planes) for z in range(planes)]
-    landings = [arrivals(z, planes, spans)[0] for z in range(planes)]
+    tables = [send_table(z, planes, spans) for z in range(planes)]
+    landings = [landing_of(z, planes, spans) for z in range(planes)]
+    parts_in = part_groups(pieces)
 
     loads = [
         pltpu.make_async_copy(cotan, cotan_held, load_sem.at[0]),
@@ -520,8 +555,8 @@
         pltpu.make_async_copy(acts.at[1], acts_held.at[1], load_sem.at[2]),
         pltpu.make_async_copy(acts.at[0], acts_held.at[0], load_sem.at[3]),
     ]
-    loads += [pltpu.make_async_copy(array, state.at[i], load_sem.at[4 + i]) for i, array in enumerate((weight, moment, second))]
-    for load in loads[:4]:
+    state_loads = [pltpu.make_async_copy(array, state.at[i], load_sem.at[4]) for i, array in enumerate((weight, moment, second))]
+    for load in loads:
         load.start()
 
     barrier = pltpu.get_barrier_semaphore()
@@ -543,18 +578,19 @@
             parts.append(jnp.where(place < counts_held[b, k], block, 0.0))
         return parts[0] if micro == 1 else jnp.concatenate(parts, axis=0)
 
-    def to_mirror(src, dst, at):
+    def to_mirror(src, dst, sent, received):
         return pltpu.make_async_remote_copy(
-            src_ref=src, dst_ref=dst, send_sem=part_send.at[at], recv_sem=part_recv.at[at],
+            src_ref=src, dst_ref=dst, send_sem=part_send.at[sent], recv_sem=part_recv.at[received],
             device_id=mirror, device_id_type=MESH)
 
-    exchange = [to_mirror(acts_out.at[at], acts_in.at[at], at) for at in range(pieces)]
-    exchange.append(to_mirror(cotan_out, cotan_in, pieces))
+    cotan_swap = to_mirror(cotan_out, cotan_in, 0, 0)
+    group_at = {at + i: g for g, (at, size) in enumerate(parts_in) for i in range(size)}
+    acts_swap = [to_mirror(acts_out.at[at], acts_in.at[at], 1, 1 + group_at[at]) for at in range(pieces)]
     loads[0].wait()
     loads[1].wait()
     cotan_out[...] = masked(1)
     pl.semaphore_wait(barrier, 1 + here[0] + here[1] + here[2])
-    exchange[pieces].start()
+    cotan_swap.start()
     rhs[0:rows, :] = masked(0).astype(jnp.bfloat16)
     for axis in range(2):
         @pl.when(here[axis] == 1)
@@ -567,7 +603,8 @@
     loads[2].wait()
 
     def run(z):
-        table, landing = tables[z], landings[z]
+        table = tables[z]
+        places, groups, unused = landings[z]
         order = ORDERS[z]
         owners = []
         for key in order:
@@ -583,15 +620,20 @@
 
         for at, owner in enumerate(owners):
             acts_out[at] = acts_held[1, :, columns(owner)].astype(jnp.float32)
-            exchange[at].start()
-        for load in loads[4:]:
+            acts_swap[at].start()
+        for load in state_loads:
             load.start()
         loads[3].wait()
-        exchange[pieces].wait_recv()
+        cotan_swap.wait_recv()
         rhs[rows:2 * rows, :] = cotan_in[...].astype(jnp.bfloat16)
+        swapped = set()
 
         def make(at):
-            exchange[at].wait_recv()
+            g = group_at[at]
+            if g not in swapped:
+                swapped.add(g)
+                part = acts_in.at[pl.ds(*parts_in[g])]
+                to_mirror(part, part, 1, 1 + g).wait_recv()
             lhs = jnp.concatenate([acts_held[0, :, columns(owners[at])], acts_in[at].astype(jnp.bfloat16)], axis=0)
             first = pl.multiple_of(owner_index(owners[at]) * piece, piece)
             grad[pl.ds(first, piece), :] = lax.dot_general(
@@ -602,22 +644,26 @@
 
         def copy_of(key):
             axis, target, needs, owner = table[key]
-            place, size, at = landings[target][key_there(key, z)]
+            place, size, at = landings[target][0][key_there(key, z)]
             device = dp + across[axis] if axis < 2 else dp + (target - z) * strides[2]
             return pltpu.make_async_remote_copy(
-                src_ref=grad.at[block(owner, spans[key[1], key[2]]), :], dst_ref=got.at[pl.ds(place, size), :],
-                send_sem=send_sem.at[sends.index(key)], recv_sem=recv_sem.at[at],
-                device_id=(device, section), device_id_type=MESH)
-
-        def arrived(key):
-            place, size, at = landing[key]
-            pltpu.make_async_remote_copy(
-                src_ref=grad.at[pl.ds(0, size), :], dst_ref=got.at[pl.ds(place, size), :],
-                send_sem=send_sem.at[0], recv_sem=recv_sem.at[at],
-                device_id=mirror, device_id_type=MESH).wait_recv()
-            return got[place:place + size, :]
-
-        sends = list(order)
+                src_ref=grad.at[block(owner, span_of(key, spans)), :], dst_ref=got.at[pl.ds(place, size), :],
+                send_sem=send_sem.at[0], recv_sem=recv_sem.at[at], device_id=(device, section), device_id_type=MESH)
+
+        landed = set()
+
+        def arrived(key, span):
+            place, size, at = places[key]
+            if at not in landed:
+                landed.add(at)
+                start = places[groups[at][0]][0]
+                whole = got.at[pl.ds(start, sum(places[k][1] for k in groups[at])), :]
+                pltpu.make_async_remote_copy(
+                    src_ref=whole, dst_ref=whole, send_sem=send_sem.at[0], recv_sem=recv_sem.at[at],
+                    device_id=mirror, device_id_type=MESH).wait_recv()
+            place += span[0] - span_of(key, spans)[0]
+            return got[place:place + span[1], :]
+
         met, done = set(), 0
         for key in order:
             axis, target, needs, owner = table[key]
@@ -625,10 +671,11 @@
                 make(done)
                 done += 1
             if needs:
-                at = block(owner, spans[key[1], key[2]])
+                span = span_of(key, spans)
+                at = block(owner, span)
                 total = grad[at, :]
                 for need in needs:
-                    total += arrived(need)
+                    total += arrived(need, span)
                 grad[at, :] = total
             if axis < 2 and axis not in met:
                 met.add(axis)
@@ -643,23 +690,24 @@
         while done < pieces:
             make(done)
             done += 1
-        for load in loads[4:]:
-            load.wait()
-        for f, c in FINALS:
+        pltpu.make_async_copy(state, state, load_sem.at[4]).wait()
+        for f, c in LASTS[z]:
             span = spans[f, c]
             total = grad[block((0, 0, z), span), :]
             for need in last_needs(f, c, z, planes):
-                total += arrived(need)
+                total += arrived(need, span)
             for part in range(per_row):
                 shard[pl.ds(span[0] * per_row + part, span[1], stride=per_row), :] = total[:, part * LANES:(part + 1) * LANES]
             flat = slice(span[0] * per_row, (span[0] + span[1]) * per_row)
             updated = adamw_shard(shard[flat, :], state[0, flat, :], state[1, flat, :], state[2, flat, :])
             for i in range(3):
                 packed[i, flat, :] = updated[i]
-        for copy in exchange:
-            copy.wait_send()
-        for key in sends:
-            copy_of(key).wait_send()
+        cotan_swap.wait_send()
+        to_mirror(acts_out, acts_in, 1, 1).wait_send()
+        sent = grad.at[pl.ds(0, sum(span_of(key, spans)[1] for key in order)), :]
+        pltpu.make_async_remote_copy(
+            src_ref=sent, dst_ref=sent, send_sem=send_sem.at[0], recv_sem=recv_sem.at[0],
+            device_id=mirror, device_id_type=MESH).wait_send()
 
     for z in range(planes):
         pl.when(here[2] == z)(functools.partial(run, z))
@@ -676,8 +724,9 @@
 def fast_fits(digits, acts, cotan, weight):
     planes, depth, width = digits[2][0], acts.shape[3], cotan.shape[3]
     piece = depth // (4 * planes)
-    total = sum(sum(chunks) for chunks in CHUNKS.values())
-    return (digits[0][0] == 2 and digits[1][0] == 2 and planes == len(ORDERS) and piece % LANES == 0 and piece % (8 * total) == 0
+    unit = spans_of(piece)
+    whole = sum(rows for (f, c), (at, rows) in unit.items() if f in "ABZ")
+    return (digits[0][0] == 2 and digits[1][0] == 2 and planes == len(ORDERS) and piece % LANES == 0 and whole == piece
             and width % LANES == 0 and piece * width == weight.shape[1])
 
 
@@ -689,10 +738,9 @@
     planes = digits[2][0]
     pieces = 4 * planes
     spans = spans_of(depth // pieces)
-    landings = [arrivals(z, planes, spans) for z in range(planes)]
-    received = max(len(slots) for slots, total in landings)
-    space = max(total for slots, total in landings)
-    sent = max(len(send_table(z, planes)) for z in range(planes))
+    landings = [landing_of(z, planes, spans) for z in range(planes)]
+    received = max(len(groups) for places, groups, total in landings)
+    space = max(total for places, groups, total in landings)
     hbm = pl.BlockSpec(memory_space=pl.ANY)
     vmem = pl.BlockSpec(memory_space=pltpu.VMEM)
     flat = (shard_rows, LANES)
@@ -714,9 +762,8 @@
             pltpu.VMEM((space, width), jnp.float32),
             pltpu.VMEM((3, *flat), jnp.float32),
             pltpu.VMEM(flat, jnp.float32),
-            pltpu.SemaphoreType.DMA((7,)), pltpu.SemaphoreType.DMA((pieces + 1,)), pltpu.SemaphoreType.DMA((pieces + 1,)),
-            pltpu.SemaphoreType.DMA((sent,)), pltpu.SemaphoreType.DMA((received,)),
-            pltpu.SemaphoreType.REGULAR((1 + planes,)),
+            pltpu.SemaphoreType.DMA((5,)), pltpu.SemaphoreType.DMA((2,)), pltpu.SemaphoreType.DMA((1 + len(part_groups(pieces)),)),
+            pltpu.SemaphoreType.DMA((1,)), pltpu.SemaphoreType.DMA((received,)), pltpu.SemaphoreType.REGULAR((1 + planes,)),
         ],
         compiler_params=pltpu.CompilerParams(collective_id=0, has_side_effects=True, vmem_limit_bytes=66 * 10**6),
         name="reduce_adamw",

time: 33.3 us -> 31.5 us (0.946)
  Pallas kernels: 32.4 us -> 30.7 us
    pallas_call x1, Pallas kernels: 31.5 us -> 29.8 us  [fast_shards(): pl.pallas_call(functools.partial(fast_kernel, digits, micro), out_shape=p...]
where the time goes in v2:
time: 31.5 us; the launch traced here: 31.3 us
  Pallas kernels  30.7 us (97%)
  between operations  0.64 us (2%)
    pallas_call x1, Pallas kernels, fast_shards(): pl.pallas_call(functools.partial(fast_kernel, digits, micro), out_shape=p...  29.8 us
    pallas_call x1, Pallas kernels, fast_shards(): pl.pallas_call(put_kernel, out_shape=(jax.ShapeDtypeStruct(flat, jnp.floa...  0.83 us

profile of v2, /device:TPU:0, one launch (start us, length us, event | category | flops | bytes accessed | tf_op | source)
XLA Modules:
  0.0 31.3 jit_solution(1155201807853189939)
XLA Ops:
  0.6 29.8 %reduce_adamw.1.packed = f32[3,384,128]{2,1,0:T(8,128)S(1)} custom-call(bf16[2,128,2048]{2,1,0:T(8,128)(2,1)} %bitcast.9, bf16[2,128,384]{2,1,0:T(8,128)(2,1)} %bitcast.10, s32[1,2]{1,0:T(1,128)} %bitcast.14, f32[384,128]{1,0:T(8,128)} %bitcast.11, f32[384,128]{1,0:T(8,128)} %bitcast.12, f32[384,128]{1,0:T(8,128)} %bitcast.13), custom_call_target="tpu_custom_call" | custom-call | tf_op jit(solution)/shard_map/reduce_adamw/pallas_call | solution.py:747
  30.5 0.8 %put.1 = (f32[384,128]{1,0:T(8,128)}, f32[384,128]{1,0:T(8,128)}, f32[384,128]{1,0:T(8,128)}) custom-call(f32[3,384,128]{2,1,0:T(8,128)S(1)} %reduce_adamw.1.packed), custom_call_target="tpu_custom_call" | custom-call | tf_op jit(solution)/shard_map/put/pallas_call | solution.py:771

commit v3 on v2

--- a/solution.py
+++ b/solution.py
@@ -10,7 +10,8 @@
 MESH = pl.DeviceIdType.MESH
 
 
-CHUNKS = {"A": (7,), "B": (6,), "Z": ((1, 2),)}
+CHUNKS = {"A": (6,), "B": (6,), "Z": ((2, 2),)}
+RELAYS = ((3, 0), (0, 3))
 LASTS = (
     (("C", 0), ("D", 0), ("A", 0), ("B", 0)),
     (("C", 0), ("D", 0), ("A", 0), ("B", 0)),
@@ -19,47 +20,48 @@
 )
 ORDERS = (
     (
-        ("1", "A", 0, 1, 2), ("z", 0, 0, 1, 3), ("1", "B", 0, 1, 1), ("z", 0, 1, 0, 3), ("z", 0, 1, 1, 3), ("z", 0, 0, 0, 3),
-        ("1", "A", 0, 1, 3), ("z", 0, 1, 1, 2), ("z", 0, 1, 0, 2), ("1", "B", 0, 1, 0), ("z", 0, 0, 0, 2), ("1", "A", 0, 0, 3),
-        ("z", 0, 1, 1, 1), ("2", "A", 0, 2), ("1", "A", 0, 1, 0), ("1", "A", 0, 1, 1), ("z", 0, 0, 1, 2), ("2", "A", 0, 3),
-        ("1", "B", 0, 1, 3), ("z", 0, 0, 1, 1), ("1", "B", 0, 1, 2), ("z", 0, 1, 0, 1), ("1", "B", 0, 0, 3), ("z", 0, 0, 0, 1),
-        ("1", "A", 0, 0, 2), ("1", "B", 0, 0, 1), ("2", "B", 0, 1), ("3", "A", 0, 3), ("2", "B", 0, 3), ("x", "D", 0, 1),
-        ("1", "B", 0, 0, 2), ("x", "C", 0, 1), ("2", "B", 0, 2), ("1", "A", 0, 0, 1), ("2", "A", 0, 1), ("3", "A", 0, 2),
-        ("2", "B", 0, 0), ("2", "A", 0, 0), ("3", "B", 0, 3), ("1", "A", 0, 0, 0), ("3", "B", 0, 1), ("y", "D", 0),
-        ("1", "B", 0, 0, 0), ("x", "C", 0, 0), ("3", "B", 0, 2), ("3", "A", 0, 1), ("x", "D", 0, 0), ("y", "C", 0),
+        ("z", 0, 1, 1, 3), ("1", "B", 0, 1, 3), ("1", "A", 0, 1, 3), ("1", "A", 0, 1, 0), ("1", "A", 0, 1, 2),
+        ("1", "B", 0, 0, 3), ("z", 0, 0, 1, 3), ("1", "A", 0, 0, 3), ("1", "B", 0, 1, 2), ("z", 0, 1, 0, 3),
+        ("1", "A", 0, 0, 2), ("z", 0, 0, 0, 3), ("z", 0, 0, 1, 2), ("z", 0, 0, 0, 2), ("1", "B", 0, 0, 1), ("z", 0, 1, 1, 2),
+        ("z", 0, 1, 0, 2), ("z", 0, 1, 0, 1), ("2", "B", 0, 3), ("z", 0, 1, 1, 1), ("1", "A", 0, 0, 1), ("1", "B", 0, 1, 0),
+        ("z", 0, 0, 1, 1), ("1", "B", 0, 1, 1), ("2", "A", 0, 2), ("1", "A", 0, 1, 1), ("2", "A", 0, 3), ("1", "B", 0, 0, 2),
+        ("z", 0, 0, 0, 1), ("2", "B", 0, 2), ("x", "C", 0, 1), ("2", "B", 0, 1), ("3", "B", 0, 3), ("1", "A", 0, 0, 0),
+        ("x", "D", 0, 1), ("1", "B", 0, 0, 0), ("3", "A", 0, 2), ("2", "A", 0, 1), ("3", "A", 0, 3), ("2", "B", 0, 0),
+        ("y", "D", 0), ("2", "A", 0, 0), ("x", "D", 0, 0), ("3", "B", 0, 2), ("y", "C", 0), ("x", "C", 0, 0), ("3", "B", 0, 1),
+        ("3", "A", 0, 1),
     ),
     (
-        ("1", "A", 0, 1, 3), ("1", "B", 0, 1, 3), ("1", "A", 0, 1, 2), ("1", "B", 0, 1, 0), ("z", 0, 0, 1, 3),
-        ("1", "A", 0, 1, 0), ("1", "B", 0, 1, 2), ("z", 0, 1, 1, 3), ("1", "A", 0, 0, 3), ("2", "A", 0, 3),
-        ("1", "B", 0, 0, 1), ("z", 0, 1, 0, 3), ("1", "B", 0, 0, 3), ("z", 0, 1, 1, 2), ("1", "A", 0, 0, 2), ("z", 0, 0, 0, 3),
-        ("2", "A", 0, 2), ("1", "B", 0, 1, 1), ("2", "B", 0, 3), ("z", 0, 1, 0, 2), ("2", "A", 0, 0), ("z", 0, 0, 0, 2),
-        ("x", "C", 0, 1), ("z", 0, 1, 1, 0), ("z", 0, 0, 1, 2), ("z", 0, 0, 0, 0), ("1", "A", 0, 0, 0), ("3", "A", 0, 3),
-        ("2", "B", 0, 2), ("z", 0, 0, 1, 0), ("x", "D", 0, 1), ("2", "B", 0, 0), ("3", "B", 0, 3), ("z", 0, 1, 0, 0),
-        ("1", "A", 0, 0, 1), ("3", "A", 0, 2), ("1", "B", 0, 0, 0), ("1", "B", 0, 0, 2), ("3", "A", 0, 0), ("1", "A", 0, 1, 1),
-        ("y", "C", 0), ("y", "D", 0), ("2", "B", 0, 1), ("x", "D", 0, 0), ("3", "B", 0, 0), ("3", "B", 0, 2), ("2", "A", 0, 1),
-        ("x", "C", 0, 0),
+        ("1", "B", 0, 1, 3), ("1", "A", 0, 1, 0), ("1", "B", 0, 1, 2), ("1", "B", 0, 1, 0), ("1", "A", 0, 1, 1),
+        ("1", "B", 0, 1, 1), ("z", 0, 1, 1, 3), ("1", "A", 0, 1, 2), ("2", "A", 0, 0), ("1", "A", 0, 0, 0),
+        ("1", "B", 0, 0, 2), ("z", 0, 0, 1, 3), ("2", "B", 0, 3), ("z", 0, 0, 0, 3), ("z", 0, 1, 0, 3), ("z", 0, 0, 1, 2),
+        ("2", "A", 0, 2), ("2", "B", 0, 2), ("1", "A", 0, 1, 3), ("z", 0, 0, 0, 2), ("1", "B", 0, 0, 0), ("z", 0, 1, 1, 0),
+        ("1", "A", 0, 0, 2), ("2", "B", 0, 0), ("z", 0, 1, 1, 2), ("z", 0, 1, 0, 0), ("z", 0, 0, 1, 0), ("1", "B", 0, 0, 3),
+        ("1", "A", 0, 0, 3), ("3", "A", 0, 0), ("z", 0, 1, 0, 2), ("x", "D", 0, 1), ("3", "B", 0, 2), ("x", "C", 0, 1),
+        ("2", "A", 0, 3), ("1", "B", 0, 0, 1), ("3", "A", 0, 2), ("x", "C", 0, 0), ("3", "B", 0, 0), ("3", "B", 0, 3),
+        ("y", "D", 0), ("1", "A", 0, 0, 1), ("x", "D", 0, 0), ("y", "C", 0), ("3", "A", 0, 3), ("2", "A", 0, 1),
+        ("z", 0, 0, 0, 0), ("2", "B", 0, 1),
     ),
     (
-        ("1", "A", 0, 1, 0), ("1", "B", 0, 1, 0), ("1", "A", 0, 0, 0), ("1", "A", 0, 1, 1), ("1", "A", 0, 1, 3),
-        ("1", "B", 0, 1, 1), ("1", "B", 0, 0, 0), ("z", 0, 1, 1, 1), ("2", "A", 0, 0), ("2", "B", 0, 0), ("z", 0, 1, 1, 0),
-        ("1", "A", 0, 1, 2), ("z", 0, 0, 0, 0), ("z", 0, 0, 1, 3), ("z", 0, 0, 1, 1), ("1", "A", 0, 0, 3), ("z", 0, 0, 1, 0),
-        ("1", "B", 0, 1, 3), ("z", 0, 1, 0, 0), ("1", "B", 0, 0, 1), ("z", 0, 1, 0, 3), ("z", 0, 1, 0, 1), ("2", "B", 0, 1),
-        ("3", "A", 0, 0), ("1", "B", 0, 0, 3), ("x", "C", 0, 1), ("z", 0, 0, 0, 1), ("2", "A", 0, 3), ("z", 0, 0, 0, 3),
-        ("x", "D", 0, 1), ("1", "A", 0, 0, 1), ("2", "A", 0, 1), ("2", "B", 0, 3), ("1", "B", 0, 1, 2), ("2", "A", 0, 2),
-        ("z", 0, 1, 1, 3), ("3", "B", 0, 0), ("3", "A", 0, 3), ("x", "D", 0, 0), ("1", "A", 0, 0, 2), ("3", "B", 0, 1),
-        ("x", "C", 0, 0), ("y", "D", 0), ("1", "B", 0, 0, 2), ("3", "B", 0, 3), ("3", "A", 0, 1), ("2", "B", 0, 2),
-        ("y", "C", 0),
+        ("1", "B", 0, 1, 1), ("1", "A", 0, 1, 1), ("1", "B", 0, 1, 3), ("1", "B", 0, 1, 0), ("1", "A", 0, 0, 0),
+        ("1", "A", 0, 1, 0), ("1", "B", 0, 0, 0), ("1", "A", 0, 0, 1), ("z", 0, 1, 1, 0), ("2", "A", 0, 1),
+        ("1", "B", 0, 0, 3), ("z", 0, 0, 1, 0), ("1", "A", 0, 1, 3), ("1", "A", 0, 1, 2), ("z", 0, 1, 0, 0), ("z", 0, 1, 1, 1),
+        ("z", 0, 0, 1, 1), ("2", "B", 0, 0), ("2", "B", 0, 3), ("z", 0, 1, 1, 3), ("2", "A", 0, 0), ("z", 0, 0, 0, 1),
+        ("2", "B", 0, 1), ("z", 0, 1, 0, 1), ("1", "B", 0, 1, 2), ("1", "B", 0, 0, 1), ("1", "A", 0, 0, 3), ("z", 0, 0, 0, 3),
+        ("2", "A", 0, 3), ("z", 0, 0, 1, 3), ("3", "A", 0, 1), ("1", "A", 0, 0, 2), ("z", 0, 0, 0, 0), ("z", 0, 1, 0, 3),
+        ("3", "B", 0, 0), ("3", "A", 0, 0), ("3", "B", 0, 3), ("x", "C", 0, 1), ("x", "D", 0, 1), ("3", "B", 0, 1),
+        ("2", "A", 0, 2), ("3", "A", 0, 3), ("2", "B", 0, 2), ("1", "B", 0, 0, 2), ("x", "C", 0, 0), ("y", "D", 0),
+        ("x", "D", 0, 0), ("y", "C", 0),
     ),
     (
-        ("z", 0, 1, 1, 1), ("1", "A", 0, 1, 0), ("1", "B", 0, 1, 0), ("1", "A", 0, 0, 0), ("1", "A", 0, 1, 1),
-        ("1", "B", 0, 1, 1), ("z", 0, 1, 1, 0), ("z", 0, 0, 0, 0), ("z", 0, 0, 1, 1), ("z", 0, 0, 1, 0), ("z", 0, 1, 0, 0),
-        ("1", "B", 0, 1, 2), ("z", 0, 1, 0, 1), ("z", 0, 0, 0, 1), ("2", "B", 0, 0), ("1", "A", 0, 1, 2), ("z", 0, 1, 1, 2),
-        ("1", "B", 0, 0, 0), ("1", "A", 0, 0, 1), ("2", "A", 0, 0), ("z", 0, 0, 1, 2), ("1", "B", 0, 0, 2), ("2", "A", 0, 1),
-        ("2", "B", 0, 2), ("1", "B", 0, 0, 1), ("3", "B", 0, 0), ("1", "A", 0, 1, 3), ("z", 0, 0, 0, 2), ("1", "B", 0, 1, 3),
-        ("3", "A", 0, 0), ("2", "B", 0, 1), ("1", "A", 0, 0, 2), ("2", "A", 0, 2), ("x", "D", 0, 0), ("z", 0, 1, 0, 2),
-        ("3", "A", 0, 1), ("x", "D", 0, 1), ("1", "B", 0, 0, 3), ("x", "C", 0, 1), ("3", "B", 0, 2), ("x", "C", 0, 0),
-        ("1", "A", 0, 0, 3), ("3", "B", 0, 1), ("2", "A", 0, 3), ("2", "B", 0, 3), ("3", "A", 0, 2), ("y", "D", 0),
-        ("y", "C", 0),
+        ("z", 0, 1, 1, 0), ("1", "B", 0, 1, 0), ("1", "A", 0, 1, 0), ("1", "B", 0, 0, 1), ("z", 0, 0, 1, 0),
+        ("1", "B", 0, 1, 1), ("z", 0, 1, 0, 0), ("1", "B", 0, 0, 0), ("1", "A", 0, 1, 2), ("z", 0, 1, 1, 1),
+        ("1", "A", 0, 1, 1), ("z", 0, 0, 1, 1), ("2", "B", 0, 0), ("2", "A", 0, 0), ("1", "B", 0, 1, 3), ("1", "B", 0, 1, 2),
+        ("z", 0, 0, 0, 1), ("1", "A", 0, 0, 0), ("2", "A", 0, 2), ("z", 0, 1, 0, 1), ("z", 0, 0, 0, 0), ("z", 0, 1, 0, 2),
+        ("1", "A", 0, 1, 3), ("1", "A", 0, 0, 1), ("1", "A", 0, 0, 2), ("2", "A", 0, 1), ("3", "B", 0, 0), ("3", "A", 0, 0),
+        ("z", 0, 1, 1, 2), ("2", "B", 0, 1), ("z", 0, 0, 0, 2), ("x", "C", 0, 1), ("x", "D", 0, 1), ("1", "B", 0, 0, 2),
+        ("z", 0, 0, 1, 2), ("1", "B", 0, 0, 3), ("2", "B", 0, 2), ("2", "B", 0, 3), ("2", "A", 0, 3), ("3", "A", 0, 2),
+        ("3", "A", 0, 1), ("y", "C", 0), ("3", "B", 0, 1), ("1", "A", 0, 0, 3), ("y", "D", 0), ("x", "C", 0, 0),
+        ("x", "D", 0, 0), ("3", "B", 0, 2),
     ),
 )
 
@@ -427,6 +429,15 @@
     return tuple(("z", c, *place, z, p) for p in planes_beside(z, planes))
 
 
+def toward(z, k):
+    return 1 if k > z else -1
+
+
+def third_needs(f, c, k, z):
+    before = z - toward(z, k)
+    return (("1", f, c, 0, k), ("2", f, c, k)) + ((("r", f, c, k, before),) if (before, k) in RELAYS else ())
+
+
 def send_table(z, planes, spans):
     table = {}
     for f, c in spans:
@@ -438,7 +449,8 @@
                     table["1", f, c, b, k] = (first, z, (), flipped(f, 1, b) + (k,))
                 table["2", f, c, k] = (second, z, (("1", f, c, 1, k),), flipped(f, 0, 1) + (k,))
                 if k != z:
-                    table["3", f, c, k] = (2, k, (("1", f, c, 0, k), ("2", f, c, k)), (0, 0, k))
+                    target = z + toward(z, k) if (z, k) in RELAYS else k
+                    table["3", f, c, k] = (2, target, third_needs(f, c, k, z), (0, 0, k))
         elif f in "CD":
             for b in range(2):
                 place = flipped(f, 1, b)
@@ -447,17 +459,17 @@
             table["y", f, c] = (second, z, crossed(c, place, z, planes) + (("x", f, c, 1),), place + (z,))
         else:
             for k in range(planes):
-                toward = 1 if k > z else -1
+                before = z - toward(z, k)
                 for a in range(2 if k != z else 0):
                     for b in range(2):
-                        needs = (("z", c, a, b, k, z - toward),) if 0 <= z - toward < planes else ()
-                        table["z", c, a, b, k] = (2, z + toward, needs, (a, b, k))
+                        needs = (("z", c, a, b, k, before),) if 0 <= before < planes else ()
+                        table["z", c, a, b, k] = (2, z + toward(z, k), needs, (a, b, k))
     return table
 
 
 def last_needs(f, c, z, planes):
     if f in "AB":
-        return (("1", f, c, 0, z), ("2", f, c, z)) + tuple(("3", f, c, p) for p in range(planes) if p != z)
+        return (("1", f, c, 0, z), ("2", f, c, z)) + tuple(("3", f, c, p) for p in range(planes) if p != z and (p, z) not in RELAYS)
     return crossed(c, (0, 0), z, planes) + (("x", f, c, 0), ("y", f, c))
 
 
@@ -467,21 +479,23 @@
         if f in "AB":
             for k in range(planes):
                 groups.append((("1", f, c, 1, k),))
-                groups.append((("1", f, c, 0, k), ("2", f, c, k)) if k != z else last_needs(f, c, z, planes))
+                groups.append(third_needs(f, c, k, z) if k != z else last_needs(f, c, z, planes))
         elif f in "CD":
             groups += [(("x", f, c, 1),), (("x", f, c, 0), ("y", f, c))]
         else:
             for place in ((0, 0), (0, 1), (1, 0), (1, 1)):
                 groups.append(crossed(c, place, z, planes))
                 for k in range(planes):
-                    before = z - 1 if k > z else z + 1
+                    before = z - toward(z, k)
                     if k != z and 0 <= before < planes:
                         groups.append((("z", c, *place, k, before),))
     return groups
 
 
 def key_there(key, z):
-    return key[:-1] + (z,) if key[0] == "3" else key + (z,) if key[0] == "z" else key
+    if key[0] == "3":
+        return ("r",) + key[1:] + (z,) if (z, key[3]) in RELAYS else key[:-1] + (z,)
+    return key + (z,) if key[0] == "z" else key
 
 
 def span_of(key, spans):
@@ -687,6 +701,9 @@
                 met.add(1 + target - z)
                 pl.semaphore_wait(up_sem.at[1 + target - z], 1)
             copy_of(key).start()
+        for step in range(1, planes - z):
+            if 1 + step not in met:
+                pl.semaphore_wait(up_sem.at[1 + step], 1)
         while done < pieces:
             make(done)
             done += 1

time: 31.5 us -> 29.8 us (0.946)
  Pallas kernels: 30.7 us -> 28.9 us
    pallas_call x1, Pallas kernels: 29.8 us -> 28.1 us  [fast_shards(): pl.pallas_call(functools.partial(fast_kernel, digits, micro), out_shape=p...]
where the time goes in v3:
time: 29.8 us; the launch traced here: 29.5 us
  Pallas kernels  28.9 us (97%)
  between operations  0.64 us (2%)
    pallas_call x1, Pallas kernels, fast_shards(): pl.pallas_call(functools.partial(fast_kernel, digits, micro), out_shape=p...  28.1 us
    pallas_call x1, Pallas kernels, fast_shards(): pl.pallas_call(put_kernel, out_shape=(jax.ShapeDtypeStruct(flat, jnp.floa...  0.83 us

profile of v3, /device:TPU:0, one launch (start us, length us, event | category | flops | bytes accessed | tf_op | source)
XLA Modules:
  0.0 29.5 jit_solution(2191727870260789057)
XLA Ops:
  0.6 28.1 %reduce_adamw.1.packed = f32[3,384,128]{2,1,0:T(8,128)S(1)} custom-call(bf16[2,128,2048]{2,1,0:T(8,128)(2,1)} %bitcast.9, bf16[2,128,384]{2,1,0:T(8,128)(2,1)} %bitcast.10, s32[1,2]{1,0:T(1,128)} %bitcast.14, f32[384,128]{1,0:T(8,128)} %bitcast.11, f32[384,128]{1,0:T(8,128)} %bitcast.12, f32[384,128]{1,0:T(8,128)} %bitcast.13), custom_call_target="tpu_custom_call" | custom-call | tf_op jit(solution)/shard_map/reduce_adamw/pallas_call | solution.py:764
  28.7 0.8 %put.1 = (f32[384,128]{1,0:T(8,128)}, f32[384,128]{1,0:T(8,128)}, f32[384,128]{1,0:T(8,128)}) custom-call(f32[3,384,128]{2,1,0:T(8,128)S(1)} %reduce_adamw.1.packed), custom_call_target="tpu_custom_call" | custom-call | tf_op jit(solution)/shard_map/put/pallas_call | solution.py:788

commit v4 on v3

--- a/solution.py
+++ b/solution.py
@@ -10,8 +10,13 @@
 MESH = pl.DeviceIdType.MESH
 
 
-CHUNKS = {"A": (6,), "B": (6,), "Z": ((2, 2),)}
-RELAYS = ((3, 0), (0, 3))
+CHUNKS = (
+    {"A": (7,), "B": (6,), "Z": ((1, 2),)},
+    {"A": (6,), "B": (6,), "Z": ((2, 2),)},
+    {"A": (6,), "B": (6,), "Z": ((2, 2),)},
+    {"A": (6,), "B": (5,), "Z": ((2, 3),)},
+)
+RELAYS = ((3, 0), (0, 3), (3, 1))
 LASTS = (
     (("C", 0), ("D", 0), ("A", 0), ("B", 0)),
     (("C", 0), ("D", 0), ("A", 0), ("B", 0)),
@@ -20,48 +25,48 @@
 )
 ORDERS = (
     (
-        ("z", 0, 1, 1, 3), ("1", "B", 0, 1, 3), ("1", "A", 0, 1, 3), ("1", "A", 0, 1, 0), ("1", "A", 0, 1, 2),
-        ("1", "B", 0, 0, 3), ("z", 0, 0, 1, 3), ("1", "A", 0, 0, 3), ("1", "B", 0, 1, 2), ("z", 0, 1, 0, 3),
-        ("1", "A", 0, 0, 2), ("z", 0, 0, 0, 3), ("z", 0, 0, 1, 2), ("z", 0, 0, 0, 2), ("1", "B", 0, 0, 1), ("z", 0, 1, 1, 2),
-        ("z", 0, 1, 0, 2), ("z", 0, 1, 0, 1), ("2", "B", 0, 3), ("z", 0, 1, 1, 1), ("1", "A", 0, 0, 1), ("1", "B", 0, 1, 0),
-        ("z", 0, 0, 1, 1), ("1", "B", 0, 1, 1), ("2", "A", 0, 2), ("1", "A", 0, 1, 1), ("2", "A", 0, 3), ("1", "B", 0, 0, 2),
-        ("z", 0, 0, 0, 1), ("2", "B", 0, 2), ("x", "C", 0, 1), ("2", "B", 0, 1), ("3", "B", 0, 3), ("1", "A", 0, 0, 0),
-        ("x", "D", 0, 1), ("1", "B", 0, 0, 0), ("3", "A", 0, 2), ("2", "A", 0, 1), ("3", "A", 0, 3), ("2", "B", 0, 0),
-        ("y", "D", 0), ("2", "A", 0, 0), ("x", "D", 0, 0), ("3", "B", 0, 2), ("y", "C", 0), ("x", "C", 0, 0), ("3", "B", 0, 1),
-        ("3", "A", 0, 1),
+        ("1", "A", 0, 1, 3), ("z", 0, 1, 1, 3), ("1", "B", 0, 1, 3), ("z", 0, 0, 1, 2), ("1", "A", 0, 1, 1),
+        ("1", "A", 0, 0, 3), ("z", 0, 0, 1, 3), ("z", 0, 0, 0, 3), ("1", "A", 0, 1, 2), ("1", "B", 0, 1, 0), ("z", 0, 1, 0, 3),
+        ("1", "B", 0, 1, 2), ("z", 0, 1, 1, 2), ("1", "B", 0, 1, 1), ("z", 0, 0, 0, 2), ("2", "B", 0, 3), ("1", "B", 0, 0, 2),
+        ("2", "B", 0, 2), ("z", 0, 1, 0, 2), ("z", 0, 0, 1, 1), ("z", 0, 1, 1, 1), ("2", "A", 0, 3), ("1", "A", 0, 1, 0),
+        ("z", 0, 1, 0, 1), ("1", "B", 0, 0, 3), ("2", "A", 0, 1), ("1", "A", 0, 0, 1), ("1", "A", 0, 0, 2),
+        ("1", "B", 0, 0, 1), ("2", "A", 0, 2), ("2", "B", 0, 1), ("3", "A", 0, 3), ("3", "B", 0, 3), ("x", "C", 0, 1),
+        ("x", "C", 0, 0), ("x", "D", 0, 1), ("1", "B", 0, 0, 0), ("2", "B", 0, 0), ("3", "B", 0, 2), ("z", 0, 0, 0, 1),
+        ("1", "A", 0, 0, 0), ("2", "A", 0, 0), ("x", "D", 0, 0), ("3", "A", 0, 1), ("3", "A", 0, 2), ("y", "C", 0),
+        ("3", "B", 0, 1), ("y", "D", 0),
     ),
     (
-        ("1", "B", 0, 1, 3), ("1", "A", 0, 1, 0), ("1", "B", 0, 1, 2), ("1", "B", 0, 1, 0), ("1", "A", 0, 1, 1),
-        ("1", "B", 0, 1, 1), ("z", 0, 1, 1, 3), ("1", "A", 0, 1, 2), ("2", "A", 0, 0), ("1", "A", 0, 0, 0),
-        ("1", "B", 0, 0, 2), ("z", 0, 0, 1, 3), ("2", "B", 0, 3), ("z", 0, 0, 0, 3), ("z", 0, 1, 0, 3), ("z", 0, 0, 1, 2),
-        ("2", "A", 0, 2), ("2", "B", 0, 2), ("1", "A", 0, 1, 3), ("z", 0, 0, 0, 2), ("1", "B", 0, 0, 0), ("z", 0, 1, 1, 0),
-        ("1", "A", 0, 0, 2), ("2", "B", 0, 0), ("z", 0, 1, 1, 2), ("z", 0, 1, 0, 0), ("z", 0, 0, 1, 0), ("1", "B", 0, 0, 3),
-        ("1", "A", 0, 0, 3), ("3", "A", 0, 0), ("z", 0, 1, 0, 2), ("x", "D", 0, 1), ("3", "B", 0, 2), ("x", "C", 0, 1),
-        ("2", "A", 0, 3), ("1", "B", 0, 0, 1), ("3", "A", 0, 2), ("x", "C", 0, 0), ("3", "B", 0, 0), ("3", "B", 0, 3),
-        ("y", "D", 0), ("1", "A", 0, 0, 1), ("x", "D", 0, 0), ("y", "C", 0), ("3", "A", 0, 3), ("2", "A", 0, 1),
-        ("z", 0, 0, 0, 0), ("2", "B", 0, 1),
+        ("1", "A", 0, 1, 2), ("1", "B", 0, 1, 2), ("1", "A", 0, 0, 2), ("1", "A", 0, 1, 0), ("1", "B", 0, 1, 3),
+        ("1", "B", 0, 1, 0), ("1", "A", 0, 0, 0), ("z", 0, 1, 1, 3), ("2", "A", 0, 2), ("1", "B", 0, 0, 0), ("z", 0, 0, 1, 2),
+        ("z", 0, 0, 1, 3), ("z", 0, 0, 0, 3), ("2", "B", 0, 0), ("1", "A", 0, 1, 3), ("2", "B", 0, 2), ("2", "A", 0, 0),
+        ("2", "B", 0, 3), ("1", "B", 0, 0, 2), ("z", 0, 1, 1, 0), ("z", 0, 1, 0, 3), ("z", 0, 1, 1, 2), ("1", "B", 0, 0, 3),
+        ("1", "B", 0, 1, 1), ("1", "A", 0, 1, 1), ("3", "A", 0, 2), ("z", 0, 0, 1, 0), ("1", "A", 0, 0, 3), ("z", 0, 0, 0, 2),
+        ("z", 0, 1, 0, 2), ("z", 0, 1, 0, 0), ("3", "A", 0, 0), ("2", "A", 0, 3), ("3", "B", 0, 0), ("3", "B", 0, 2),
+        ("x", "C", 0, 1), ("1", "A", 0, 0, 1), ("x", "D", 0, 0), ("x", "C", 0, 0), ("z", 0, 0, 0, 0), ("x", "D", 0, 1),
+        ("2", "A", 0, 1), ("2", "B", 0, 1), ("1", "B", 0, 0, 1), ("3", "B", 0, 3), ("3", "A", 0, 3), ("y", "D", 0),
+        ("y", "C", 0),
     ),
     (
-        ("1", "B", 0, 1, 1), ("1", "A", 0, 1, 1), ("1", "B", 0, 1, 3), ("1", "B", 0, 1, 0), ("1", "A", 0, 0, 0),
-        ("1", "A", 0, 1, 0), ("1", "B", 0, 0, 0), ("1", "A", 0, 0, 1), ("z", 0, 1, 1, 0), ("2", "A", 0, 1),
-        ("1", "B", 0, 0, 3), ("z", 0, 0, 1, 0), ("1", "A", 0, 1, 3), ("1", "A", 0, 1, 2), ("z", 0, 1, 0, 0), ("z", 0, 1, 1, 1),
-        ("z", 0, 0, 1, 1), ("2", "B", 0, 0), ("2", "B", 0, 3), ("z", 0, 1, 1, 3), ("2", "A", 0, 0), ("z", 0, 0, 0, 1),
-        ("2", "B", 0, 1), ("z", 0, 1, 0, 1), ("1", "B", 0, 1, 2), ("1", "B", 0, 0, 1), ("1", "A", 0, 0, 3), ("z", 0, 0, 0, 3),
-        ("2", "A", 0, 3), ("z", 0, 0, 1, 3), ("3", "A", 0, 1), ("1", "A", 0, 0, 2), ("z", 0, 0, 0, 0), ("z", 0, 1, 0, 3),
-        ("3", "B", 0, 0), ("3", "A", 0, 0), ("3", "B", 0, 3), ("x", "C", 0, 1), ("x", "D", 0, 1), ("3", "B", 0, 1),
-        ("2", "A", 0, 2), ("3", "A", 0, 3), ("2", "B", 0, 2), ("1", "B", 0, 0, 2), ("x", "C", 0, 0), ("y", "D", 0),
-        ("x", "D", 0, 0), ("y", "C", 0),
+        ("1", "B", 0, 0, 3), ("1", "B", 0, 1, 0), ("1", "A", 0, 1, 1), ("1", "B", 0, 1, 3), ("1", "B", 0, 1, 1),
+        ("1", "A", 0, 1, 0), ("1", "B", 0, 0, 0), ("1", "B", 0, 1, 2), ("z", 0, 1, 1, 0), ("1", "A", 0, 1, 2),
+        ("1", "A", 0, 1, 3), ("z", 0, 0, 1, 0), ("2", "A", 0, 0), ("1", "B", 0, 0, 1), ("2", "B", 0, 3), ("z", 0, 1, 0, 0),
+        ("2", "A", 0, 1), ("1", "A", 0, 0, 0), ("z", 0, 1, 1, 3), ("z", 0, 0, 0, 0), ("z", 0, 1, 1, 1), ("2", "B", 0, 0),
+        ("2", "A", 0, 3), ("z", 0, 0, 1, 1), ("2", "B", 0, 1), ("z", 0, 0, 1, 3), ("1", "A", 0, 0, 3), ("x", "D", 0, 1),
+        ("x", "C", 0, 1), ("z", 0, 1, 0, 3), ("z", 0, 1, 0, 1), ("z", 0, 0, 0, 1), ("2", "A", 0, 2), ("3", "B", 0, 3),
+        ("1", "A", 0, 0, 1), ("3", "A", 0, 0), ("z", 0, 0, 0, 3), ("3", "B", 0, 0), ("1", "A", 0, 0, 2), ("1", "B", 0, 0, 2),
+        ("3", "B", 0, 1), ("2", "B", 0, 2), ("3", "A", 0, 3), ("x", "D", 0, 0), ("y", "D", 0), ("x", "C", 0, 0),
+        ("3", "A", 0, 1), ("y", "C", 0),
     ),
     (
-        ("z", 0, 1, 1, 0), ("1", "B", 0, 1, 0), ("1", "A", 0, 1, 0), ("1", "B", 0, 0, 1), ("z", 0, 0, 1, 0),
-        ("1", "B", 0, 1, 1), ("z", 0, 1, 0, 0), ("1", "B", 0, 0, 0), ("1", "A", 0, 1, 2), ("z", 0, 1, 1, 1),
-        ("1", "A", 0, 1, 1), ("z", 0, 0, 1, 1), ("2", "B", 0, 0), ("2", "A", 0, 0), ("1", "B", 0, 1, 3), ("1", "B", 0, 1, 2),
-        ("z", 0, 0, 0, 1), ("1", "A", 0, 0, 0), ("2", "A", 0, 2), ("z", 0, 1, 0, 1), ("z", 0, 0, 0, 0), ("z", 0, 1, 0, 2),
-        ("1", "A", 0, 1, 3), ("1", "A", 0, 0, 1), ("1", "A", 0, 0, 2), ("2", "A", 0, 1), ("3", "B", 0, 0), ("3", "A", 0, 0),
-        ("z", 0, 1, 1, 2), ("2", "B", 0, 1), ("z", 0, 0, 0, 2), ("x", "C", 0, 1), ("x", "D", 0, 1), ("1", "B", 0, 0, 2),
-        ("z", 0, 0, 1, 2), ("1", "B", 0, 0, 3), ("2", "B", 0, 2), ("2", "B", 0, 3), ("2", "A", 0, 3), ("3", "A", 0, 2),
-        ("3", "A", 0, 1), ("y", "C", 0), ("3", "B", 0, 1), ("1", "A", 0, 0, 3), ("y", "D", 0), ("x", "C", 0, 0),
-        ("x", "D", 0, 0), ("3", "B", 0, 2),
+        ("z", 0, 1, 1, 0), ("1", "B", 0, 1, 0), ("1", "A", 0, 1, 0), ("1", "B", 0, 0, 0), ("z", 0, 1, 0, 0),
+        ("1", "A", 0, 0, 0), ("z", 0, 1, 1, 1), ("1", "A", 0, 1, 1), ("z", 0, 0, 1, 0), ("z", 0, 0, 0, 1), ("1", "B", 0, 1, 1),
+        ("1", "A", 0, 1, 2), ("z", 0, 1, 1, 2), ("z", 0, 0, 0, 0), ("z", 0, 0, 1, 1), ("2", "A", 0, 0), ("1", "B", 0, 1, 2),
+        ("1", "B", 0, 1, 3), ("2", "B", 0, 0), ("z", 0, 1, 0, 1), ("z", 0, 1, 0, 2), ("2", "B", 0, 1), ("3", "A", 0, 0),
+        ("z", 0, 0, 1, 2), ("1", "B", 0, 0, 1), ("2", "A", 0, 1), ("1", "A", 0, 0, 1), ("x", "C", 0, 1), ("1", "A", 0, 0, 2),
+        ("2", "B", 0, 2), ("3", "B", 0, 0), ("2", "A", 0, 2), ("1", "B", 0, 0, 2), ("3", "B", 0, 1), ("1", "A", 0, 1, 3),
+        ("1", "A", 0, 0, 3), ("3", "A", 0, 1), ("x", "D", 0, 1), ("y", "C", 0), ("x", "C", 0, 0), ("3", "A", 0, 2),
+        ("1", "B", 0, 0, 3), ("2", "B", 0, 3), ("3", "B", 0, 2), ("x", "D", 0, 0), ("z", 0, 0, 0, 2), ("2", "A", 0, 3),
+        ("y", "D", 0),
     ),
 )
 
@@ -440,7 +445,7 @@
 
 def send_table(z, planes, spans):
     table = {}
-    for f, c in spans:
+    for f, c in spans[z]:
         if f in AXES:
             first, second = AXES[f]
         if f in "AB":
@@ -475,7 +480,7 @@
 
 def wait_groups(z, planes, spans):
     groups = []
-    for f, c in spans:
+    for f, c in spans[z]:
         if f in "AB":
             for k in range(planes):
                 groups.append((("1", f, c, 1, k),))
@@ -498,33 +503,38 @@
     return key + (z,) if key[0] == "z" else key
 
 
-def span_of(key, spans):
-    return spans[("Z",) + key[1:2]] if key[0] == "z" else spans[key[1], key[2]]
+def span_of(key, spans, z, coming):
+    if key[0] in "xy" or key[0] == "3" and coming:
+        k = z
+    else:
+        k = key[4 if key[0] in "1z" else 3]
+    return spans[k][("Z", key[1]) if key[0] == "z" else key[1:3]]
 
 
 def spans_of(piece):
-    total = sum(CHUNKS["A"]) + sum(CHUNKS["B"]) + sum(sum(pair) for pair in CHUNKS["Z"])
-    unit = piece // 8 // total * 8
-    spans, at = {}, 0
-    for f in "AB":
-        for c, size in enumerate(CHUNKS[f]):
-            spans[f, c] = (at, size * unit)
-            at += size * unit
-    for c, (first, second) in enumerate(CHUNKS["Z"]):
-        spans["Z", c] = (at, (first + second) * unit)
-        if first:
+    planes = []
+    for chunks in CHUNKS:
+        total = sum(chunks["A"]) + sum(chunks["B"]) + sum(sum(pair) for pair in chunks["Z"])
+        unit = piece // 8 // total * 8
+        spans, at = {}, 0
+        for f in "AB":
+            for c, size in enumerate(chunks[f]):
+                spans[f, c] = (at, size * unit)
+                at += size * unit
+        for c, (first, second) in enumerate(chunks["Z"]):
+            spans["Z", c] = (at, (first + second) * unit)
             spans["C", c] = (at, first * unit)
-        if second:
             spans["D", c] = (at + first * unit, second * unit)
-        at += (first + second) * unit
-    return spans
+            at += (first + second) * unit
+        planes.append(spans)
+    return planes
 
 
 def landing_of(z, planes, spans):
     places, at, groups = {}, 0, wait_groups(z, planes, spans)
     for i, group in enumerate(groups):
         for key in group:
-            rows = span_of(key, spans)[1]
+            rows = span_of(key, spans, z, True)[1]
             places[key] = (at, rows, i)
             at += rows
     return places, groups, at
@@ -661,7 +671,7 @@
             place, size, at = landings[target][0][key_there(key, z)]
             device = dp + across[axis] if axis < 2 else dp + (target - z) * strides[2]
             return pltpu.make_async_remote_copy(
-                src_ref=grad.at[block(owner, span_of(key, spans)), :], dst_ref=got.at[pl.ds(place, size), :],
+                src_ref=grad.at[block(owner, span_of(key, spans, z, False)), :], dst_ref=got.at[pl.ds(place, size), :],
                 send_sem=send_sem.at[0], recv_sem=recv_sem.at[at], device_id=(device, section), device_id_type=MESH)
 
         landed = set()
@@ -675,7 +685,7 @@
                 pltpu.make_async_remote_copy(
                     src_ref=whole, dst_ref=whole, send_sem=send_sem.at[0], recv_sem=recv_sem.at[at],
                     device_id=mirror, device_id_type=MESH).wait_recv()
-            place += span[0] - span_of(key, spans)[0]
+            place += span[0] - span_of(key, spans, z, True)[0]
             return got[place:place + span[1], :]
 
         met, done = set(), 0
@@ -685,7 +695,7 @@
                 make(done)
                 done += 1
             if needs:
-                span = span_of(key, spans)
+                span = span_of(key, spans, z, False)
                 at = block(owner, span)
                 total = grad[at, :]
                 for need in needs:
@@ -709,7 +719,7 @@
             done += 1
         pltpu.make_async_copy(state, state, load_sem.at[4]).wait()
         for f, c in LASTS[z]:
-            span = spans[f, c]
+            span = spans[z][f, c]
             total = grad[block((0, 0, z), span), :]
             for need in last_needs(f, c, z, planes):
                 total += arrived(need, span)
@@ -721,7 +731,7 @@
                 packed[i, flat, :] = updated[i]
         cotan_swap.wait_send()
         to_mirror(acts_out, acts_in, 1, 1).wait_send()
-        sent = grad.at[pl.ds(0, sum(span_of(key, spans)[1] for key in order)), :]
+        sent = grad.at[pl.ds(0, sum(span_of(key, spans, z, False)[1] for key in order)), :]
         pltpu.make_async_remote_copy(
             src_ref=sent, dst_ref=sent, send_sem=send_sem.at[0], recv_sem=recv_sem.at[0],
             device_id=mirror, device_id_type=MESH).wait_send()
@@ -741,9 +751,8 @@
 def fast_fits(digits, acts, cotan, weight):
     planes, depth, width = digits[2][0], acts.shape[3], cotan.shape[3]
     piece = depth // (4 * planes)
-    unit = spans_of(piece)
-    whole = sum(rows for (f, c), (at, rows) in unit.items() if f in "ABZ")
-    return (digits[0][0] == 2 and digits[1][0] == 2 and planes == len(ORDERS) and piece % LANES == 0 and whole == piece
+    whole = all(sum(rows for (f, c), (at, rows) in spans.items() if f in "ABZ") == piece for spans in spans_of(piece))
+    return (digits[0][0] == 2 and digits[1][0] == 2 and planes == len(ORDERS) and piece % LANES == 0 and whole
             and width % LANES == 0 and piece * width == weight.shape[1])
 
 

time: 29.8 us -> 29.3 us (0.983)
  Pallas kernels: 28.9 us -> 28.5 us
    pallas_call x1, Pallas kernels: 28.1 us -> 27.6 us  [fast_shards(): pl.pallas_call(functools.partial(fast_kernel, digits, micro), out_shape=p...]
where the time goes in v4:
time: 29.3 us; the launch traced here: 29.1 us
  Pallas kernels  28.5 us (97%)
  between operations  0.64 us (2%)
    pallas_call x1, Pallas kernels, fast_shards(): pl.pallas_call(functools.partial(fast_kernel, digits, micro), out_shape=p...  27.6 us
    pallas_call x1, Pallas kernels, fast_shards(): pl.pallas_call(put_kernel, out_shape=(jax.ShapeDtypeStruct(flat, jnp.floa...  0.83 us

profile of v4, /device:TPU:0, one launch (start us, length us, event | category | flops | bytes accessed | tf_op | source)
XLA Modules:
  0.0 29.1 jit_solution(8091917407135933643)
XLA Ops:
  0.6 27.6 %reduce_adamw.1.packed = f32[3,384,128]{2,1,0:T(8,128)S(1)} custom-call(bf16[2,128,2048]{2,1,0:T(8,128)(2,1)} %bitcast.9, bf16[2,128,384]{2,1,0:T(8,128)(2,1)} %bitcast.10, s32[1,2]{1,0:T(1,128)} %bitcast.14, f32[384,128]{1,0:T(8,128)} %bitcast.11, f32[384,128]{1,0:T(8,128)} %bitcast.12, f32[384,128]{1,0:T(8,128)} %bitcast.13), custom_call_target="tpu_custom_call" | custom-call | tf_op jit(solution)/shard_map/reduce_adamw/pallas_call | solution.py:773
  28.3 0.8 %put.1 = (f32[384,128]{1,0:T(8,128)}, f32[384,128]{1,0:T(8,128)}, f32[384,128]{1,0:T(8,128)}) custom-call(f32[3,384,128]{2,1,0:T(8,128)S(1)} %reduce_adamw.1.packed), custom_call_target="tpu_custom_call" | custom-call | tf_op jit(solution)/shard_map/put/pallas_call | solution.py:797

commit v5 on v4

--- a/solution.py
+++ b/solution.py
@@ -16,57 +16,56 @@
     {"A": (6,), "B": (6,), "Z": ((2, 2),)},
     {"A": (6,), "B": (5,), "Z": ((2, 3),)},
 )
-RELAYS = ((3, 0), (0, 3), (3, 1))
+RELAYS = ((3, 1), (3, 0), (0, 2), (0, 3))
 LASTS = (
-    (("C", 0), ("D", 0), ("A", 0), ("B", 0)),
-    (("C", 0), ("D", 0), ("A", 0), ("B", 0)),
-    (("C", 0), ("D", 0), ("A", 0), ("B", 0)),
-    (("C", 0), ("D", 0), ("A", 0), ("B", 0)),
+    (("A", 0), ("C", 0), ("B", 0), ("D", 0)),
+    (("D", 0), ("C", 0), ("B", 0), ("A", 0)),
+    (("A", 0), ("C", 0), ("D", 0), ("B", 0)),
+    (("D", 0), ("A", 0), ("C", 0), ("B", 0)),
 )
 ORDERS = (
     (
-        ("1", "A", 0, 1, 3), ("z", 0, 1, 1, 3), ("1", "B", 0, 1, 3), ("z", 0, 0, 1, 2), ("1", "A", 0, 1, 1),
-        ("1", "A", 0, 0, 3), ("z", 0, 0, 1, 3), ("z", 0, 0, 0, 3), ("1", "A", 0, 1, 2), ("1", "B", 0, 1, 0), ("z", 0, 1, 0, 3),
-        ("1", "B", 0, 1, 2), ("z", 0, 1, 1, 2), ("1", "B", 0, 1, 1), ("z", 0, 0, 0, 2), ("2", "B", 0, 3), ("1", "B", 0, 0, 2),
-        ("2", "B", 0, 2), ("z", 0, 1, 0, 2), ("z", 0, 0, 1, 1), ("z", 0, 1, 1, 1), ("2", "A", 0, 3), ("1", "A", 0, 1, 0),
-        ("z", 0, 1, 0, 1), ("1", "B", 0, 0, 3), ("2", "A", 0, 1), ("1", "A", 0, 0, 1), ("1", "A", 0, 0, 2),
-        ("1", "B", 0, 0, 1), ("2", "A", 0, 2), ("2", "B", 0, 1), ("3", "A", 0, 3), ("3", "B", 0, 3), ("x", "C", 0, 1),
-        ("x", "C", 0, 0), ("x", "D", 0, 1), ("1", "B", 0, 0, 0), ("2", "B", 0, 0), ("3", "B", 0, 2), ("z", 0, 0, 0, 1),
-        ("1", "A", 0, 0, 0), ("2", "A", 0, 0), ("x", "D", 0, 0), ("3", "A", 0, 1), ("3", "A", 0, 2), ("y", "C", 0),
-        ("3", "B", 0, 1), ("y", "D", 0),
+        ("1", "A", 0, 1, 2), ("z", 0, 1, 1, 2), ("1", "B", 0, 1, 2), ("1", "A", 0, 1, 3), ("z", 0, 1, 0, 3),
+        ("1", "B", 0, 1, 3), ("1", "A", 0, 1, 1), ("z", 0, 1, 1, 3), ("z", 0, 0, 0, 2), ("1", "A", 0, 0, 3), ("z", 0, 0, 1, 3),
+        ("1", "B", 0, 0, 3), ("1", "B", 0, 1, 1), ("1", "B", 0, 0, 1), ("1", "A", 0, 0, 2), ("z", 0, 1, 0, 2),
+        ("2", "A", 0, 3), ("z", 0, 0, 0, 3), ("2", "B", 0, 3), ("2", "A", 0, 2), ("1", "A", 0, 1, 0), ("2", "B", 0, 2),
+        ("z", 0, 0, 1, 2), ("z", 0, 1, 0, 1), ("z", 0, 0, 1, 1), ("z", 0, 1, 1, 1), ("1", "B", 0, 1, 0), ("1", "B", 0, 0, 2),
+        ("x", "D", 0, 1), ("x", "C", 0, 1), ("3", "A", 0, 3), ("2", "B", 0, 1), ("1", "A", 0, 0, 0), ("3", "B", 0, 3),
+        ("x", "C", 0, 0), ("2", "A", 0, 1), ("1", "A", 0, 0, 1), ("2", "B", 0, 0), ("2", "A", 0, 0), ("3", "A", 0, 2),
+        ("3", "B", 0, 2), ("3", "B", 0, 1), ("y", "C", 0), ("y", "D", 0), ("x", "D", 0, 0), ("1", "B", 0, 0, 0),
+        ("z", 0, 0, 0, 1), ("3", "A", 0, 1),
     ),
     (
-        ("1", "A", 0, 1, 2), ("1", "B", 0, 1, 2), ("1", "A", 0, 0, 2), ("1", "A", 0, 1, 0), ("1", "B", 0, 1, 3),
-        ("1", "B", 0, 1, 0), ("1", "A", 0, 0, 0), ("z", 0, 1, 1, 3), ("2", "A", 0, 2), ("1", "B", 0, 0, 0), ("z", 0, 0, 1, 2),
-        ("z", 0, 0, 1, 3), ("z", 0, 0, 0, 3), ("2", "B", 0, 0), ("1", "A", 0, 1, 3), ("2", "B", 0, 2), ("2", "A", 0, 0),
-        ("2", "B", 0, 3), ("1", "B", 0, 0, 2), ("z", 0, 1, 1, 0), ("z", 0, 1, 0, 3), ("z", 0, 1, 1, 2), ("1", "B", 0, 0, 3),
-        ("1", "B", 0, 1, 1), ("1", "A", 0, 1, 1), ("3", "A", 0, 2), ("z", 0, 0, 1, 0), ("1", "A", 0, 0, 3), ("z", 0, 0, 0, 2),
-        ("z", 0, 1, 0, 2), ("z", 0, 1, 0, 0), ("3", "A", 0, 0), ("2", "A", 0, 3), ("3", "B", 0, 0), ("3", "B", 0, 2),
-        ("x", "C", 0, 1), ("1", "A", 0, 0, 1), ("x", "D", 0, 0), ("x", "C", 0, 0), ("z", 0, 0, 0, 0), ("x", "D", 0, 1),
-        ("2", "A", 0, 1), ("2", "B", 0, 1), ("1", "B", 0, 0, 1), ("3", "B", 0, 3), ("3", "A", 0, 3), ("y", "D", 0),
-        ("y", "C", 0),
+        ("1", "B", 0, 1, 3), ("1", "A", 0, 1, 3), ("1", "A", 0, 1, 0), ("1", "B", 0, 1, 0), ("1", "A", 0, 0, 0),
+        ("1", "B", 0, 1, 2), ("1", "B", 0, 1, 1), ("z", 0, 1, 1, 2), ("z", 0, 1, 1, 3), ("1", "B", 0, 0, 0), ("2", "B", 0, 0),
+        ("1", "A", 0, 1, 2), ("z", 0, 0, 0, 2), ("z", 0, 1, 0, 3), ("2", "B", 0, 2), ("z", 0, 1, 1, 0), ("2", "A", 0, 0),
+        ("2", "A", 0, 3), ("z", 0, 0, 1, 3), ("1", "A", 0, 0, 3), ("z", 0, 1, 0, 0), ("z", 0, 0, 0, 3), ("2", "B", 0, 3),
+        ("z", 0, 1, 0, 2), ("1", "B", 0, 0, 3), ("3", "B", 0, 0), ("1", "A", 0, 0, 2), ("2", "A", 0, 2), ("1", "A", 0, 1, 1),
+        ("z", 0, 0, 1, 2), ("3", "A", 0, 0), ("z", 0, 0, 1, 0), ("1", "B", 0, 0, 2), ("3", "A", 0, 3), ("x", "D", 0, 1),
+        ("x", "C", 0, 1), ("1", "A", 0, 0, 1), ("z", 0, 0, 0, 0), ("x", "D", 0, 0), ("3", "B", 0, 3), ("1", "B", 0, 0, 1),
+        ("x", "C", 0, 0), ("3", "A", 0, 2), ("2", "B", 0, 1), ("2", "A", 0, 1), ("y", "D", 0), ("y", "C", 0), ("3", "B", 0, 2),
     ),
     (
-        ("1", "B", 0, 0, 3), ("1", "B", 0, 1, 0), ("1", "A", 0, 1, 1), ("1", "B", 0, 1, 3), ("1", "B", 0, 1, 1),
-        ("1", "A", 0, 1, 0), ("1", "B", 0, 0, 0), ("1", "B", 0, 1, 2), ("z", 0, 1, 1, 0), ("1", "A", 0, 1, 2),
-        ("1", "A", 0, 1, 3), ("z", 0, 0, 1, 0), ("2", "A", 0, 0), ("1", "B", 0, 0, 1), ("2", "B", 0, 3), ("z", 0, 1, 0, 0),
-        ("2", "A", 0, 1), ("1", "A", 0, 0, 0), ("z", 0, 1, 1, 3), ("z", 0, 0, 0, 0), ("z", 0, 1, 1, 1), ("2", "B", 0, 0),
-        ("2", "A", 0, 3), ("z", 0, 0, 1, 1), ("2", "B", 0, 1), ("z", 0, 0, 1, 3), ("1", "A", 0, 0, 3), ("x", "D", 0, 1),
-        ("x", "C", 0, 1), ("z", 0, 1, 0, 3), ("z", 0, 1, 0, 1), ("z", 0, 0, 0, 1), ("2", "A", 0, 2), ("3", "B", 0, 3),
-        ("1", "A", 0, 0, 1), ("3", "A", 0, 0), ("z", 0, 0, 0, 3), ("3", "B", 0, 0), ("1", "A", 0, 0, 2), ("1", "B", 0, 0, 2),
-        ("3", "B", 0, 1), ("2", "B", 0, 2), ("3", "A", 0, 3), ("x", "D", 0, 0), ("y", "D", 0), ("x", "C", 0, 0),
-        ("3", "A", 0, 1), ("y", "C", 0),
+        ("1", "A", 0, 1, 2), ("1", "B", 0, 1, 0), ("1", "A", 0, 1, 0), ("1", "B", 0, 1, 1), ("1", "A", 0, 1, 3),
+        ("1", "A", 0, 0, 0), ("1", "B", 0, 0, 3), ("1", "A", 0, 1, 1), ("2", "B", 0, 0), ("1", "B", 0, 1, 2),
+        ("z", 0, 1, 1, 0), ("1", "B", 0, 1, 3), ("1", "A", 0, 0, 1), ("2", "B", 0, 1), ("z", 0, 1, 0, 0), ("z", 0, 0, 0, 1),
+        ("2", "A", 0, 3), ("x", "D", 0, 1), ("2", "A", 0, 0), ("z", 0, 1, 1, 3), ("z", 0, 1, 0, 1), ("z", 0, 0, 1, 0),
+        ("z", 0, 1, 0, 3), ("1", "B", 0, 0, 0), ("2", "B", 0, 3), ("2", "A", 0, 1), ("1", "A", 0, 0, 3), ("z", 0, 0, 1, 1),
+        ("z", 0, 1, 1, 1), ("z", 0, 0, 0, 0), ("z", 0, 0, 1, 3), ("z", 0, 0, 0, 3), ("x", "C", 0, 1), ("1", "B", 0, 0, 1),
+        ("2", "B", 0, 2), ("1", "B", 0, 0, 2), ("1", "A", 0, 0, 2), ("3", "A", 0, 0), ("x", "D", 0, 0), ("3", "B", 0, 0),
+        ("3", "B", 0, 3), ("x", "C", 0, 0), ("2", "A", 0, 2), ("3", "A", 0, 1), ("3", "B", 0, 1), ("3", "A", 0, 3),
+        ("y", "C", 0), ("y", "D", 0),
     ),
     (
-        ("z", 0, 1, 1, 0), ("1", "B", 0, 1, 0), ("1", "A", 0, 1, 0), ("1", "B", 0, 0, 0), ("z", 0, 1, 0, 0),
-        ("1", "A", 0, 0, 0), ("z", 0, 1, 1, 1), ("1", "A", 0, 1, 1), ("z", 0, 0, 1, 0), ("z", 0, 0, 0, 1), ("1", "B", 0, 1, 1),
-        ("1", "A", 0, 1, 2), ("z", 0, 1, 1, 2), ("z", 0, 0, 0, 0), ("z", 0, 0, 1, 1), ("2", "A", 0, 0), ("1", "B", 0, 1, 2),
-        ("1", "B", 0, 1, 3), ("2", "B", 0, 0), ("z", 0, 1, 0, 1), ("z", 0, 1, 0, 2), ("2", "B", 0, 1), ("3", "A", 0, 0),
-        ("z", 0, 0, 1, 2), ("1", "B", 0, 0, 1), ("2", "A", 0, 1), ("1", "A", 0, 0, 1), ("x", "C", 0, 1), ("1", "A", 0, 0, 2),
-        ("2", "B", 0, 2), ("3", "B", 0, 0), ("2", "A", 0, 2), ("1", "B", 0, 0, 2), ("3", "B", 0, 1), ("1", "A", 0, 1, 3),
-        ("1", "A", 0, 0, 3), ("3", "A", 0, 1), ("x", "D", 0, 1), ("y", "C", 0), ("x", "C", 0, 0), ("3", "A", 0, 2),
-        ("1", "B", 0, 0, 3), ("2", "B", 0, 3), ("3", "B", 0, 2), ("x", "D", 0, 0), ("z", 0, 0, 0, 2), ("2", "A", 0, 3),
-        ("y", "D", 0),
+        ("z", 0, 1, 1, 0), ("1", "B", 0, 1, 0), ("1", "A", 0, 1, 0), ("1", "B", 0, 0, 1), ("z", 0, 1, 0, 0),
+        ("1", "A", 0, 1, 1), ("z", 0, 0, 0, 1), ("z", 0, 0, 1, 0), ("1", "A", 0, 0, 0), ("z", 0, 1, 1, 2), ("1", "B", 0, 1, 1),
+        ("z", 0, 1, 0, 1), ("z", 0, 0, 1, 1), ("2", "A", 0, 0), ("z", 0, 0, 1, 2), ("2", "B", 0, 0), ("1", "A", 0, 0, 1),
+        ("z", 0, 1, 1, 1), ("1", "A", 0, 1, 2), ("1", "B", 0, 0, 0), ("2", "A", 0, 1), ("z", 0, 0, 0, 0), ("2", "B", 0, 1),
+        ("1", "A", 0, 1, 3), ("1", "B", 0, 1, 2), ("1", "A", 0, 0, 2), ("3", "A", 0, 0), ("1", "B", 0, 0, 2), ("3", "B", 0, 0),
+        ("z", 0, 1, 0, 2), ("3", "A", 0, 1), ("2", "A", 0, 2), ("2", "B", 0, 2), ("x", "D", 0, 1), ("3", "B", 0, 1),
+        ("x", "C", 0, 1), ("1", "B", 0, 1, 3), ("1", "A", 0, 0, 3), ("2", "A", 0, 3), ("z", 0, 0, 0, 2), ("3", "A", 0, 2),
+        ("y", "D", 0), ("1", "B", 0, 0, 3), ("3", "B", 0, 2), ("x", "C", 0, 0), ("x", "D", 0, 0), ("2", "B", 0, 3),
+        ("y", "C", 0),
     ),
 )
 

time: 29.3 us -> 29.2 us (level)
  no operation moved by 1% of the time
where the time goes in v5:
time: 29.2 us; the launch traced here: 28.9 us
  Pallas kernels  28.3 us (97%)
  between operations  0.64 us (2%)
    pallas_call x1, Pallas kernels, fast_shards(): pl.pallas_call(functools.partial(fast_kernel, digits, micro), out_shape=p...  27.4 us
    pallas_call x1, Pallas kernels, fast_shards(): pl.pallas_call(put_kernel, out_shape=(jax.ShapeDtypeStruct(flat, jnp.floa...  0.83 us

profile of v5, /device:TPU:0, one launch (start us, length us, event | category | flops | bytes accessed | tf_op | source)
XLA Modules:
  0.0 28.9 jit_solution(9808045427491316078)
XLA Ops:
  0.6 27.4 %reduce_adamw.1.packed = f32[3,384,128]{2,1,0:T(8,128)S(1)} custom-call(bf16[2,128,2048]{2,1,0:T(8,128)(2,1)} %bitcast.9, bf16[2,128,384]{2,1,0:T(8,128)(2,1)} %bitcast.10, s32[1,2]{1,0:T(1,128)} %bitcast.14, f32[384,128]{1,0:T(8,128)} %bitcast.11, f32[384,128]{1,0:T(8,128)} %bitcast.12, f32[384,128]{1,0:T(8,128)} %bitcast.13), custom_call_target="tpu_custom_call" | custom-call | tf_op jit(solution)/shard_map/reduce_adamw/pallas_call | solution.py:772
  28.1 0.8 %put.1 = (f32[384,128]{1,0:T(8,128)}, f32[384,128]{1,0:T(8,128)}, f32[384,128]{1,0:T(8,128)}) custom-call(f32[3,384,128]{2,1,0:T(8,128)S(1)} %reduce_adamw.1.packed), custom_call_target="tpu_custom_call" | custom-call | tf_op jit(solution)/shard_map/put/pallas_call | solution.py:796
